TPU v7x, 1024 devices: a whole 8x8x8 slice. The times are simulated.
1024 devices in a mesh: lat: 64 (over z, y), lon: 16 (over x, core).
Axes of the slice: x: 8, y: 8, z: 8, core: 2. Of those that a mesh axis runs over, the one named last changes fastest.
Arguments:
- spec: float32 [4, 2, 640, 1344], P(None, None, 'lat', 'lon'), may hold values from -6 to 6
- legendre: bfloat16 [640, 1344, 1280], P('lat', 'lon'), may hold values from -0.25 to 0.25
- wave_pairs: int32 [640], replicated, may hold values from 0 to 639, each once
- row_waves: int32 [2560], P('lat'), may hold values from 16 to 1280, as said below
- forcing: float32 [4, 2560, 5120], P(None, 'lat', 'lon'), may hold values from -6 to 6
- helm_coef: float32 [4], replicated, may hold values from 6.1035155e-07 to 4.8828124e-06
Outputs:
- grid_field: float32 [4, 2560, 5120], P(None, 'lat', 'lon')
- spec_new: float32 [4, 2, 640, 1344], P(None, None, 'lat', 'lon')
Inputs may be any that keep to these rules, and one draw needn't show every extreme that they name: Each value appears once; row s holds the wavenumbers wave_pairs[s] and 1279 - wave_pairs[s]. `row_waves`: rows near the equator resolve all 1280 wavenumbers.
All inputs are finite; a program needn't handle non-finite values.
Results may differ from a plain program's by a relative error of at most 0.028.
Values may be sent and summed in bfloat16 or wider, within the bound.
A program may use at most 64 MiB of HBM per device.

v0:
```python
import math

import jax
import jax.numpy as jnp
from jax import lax
from jax.sharding import PartitionSpec as P

M = 1280


def cut_along(x, dim, size):
    before, after = (x.shape[:dim], x.shape[dim + 1 :])
    return jnp.moveaxis(x.reshape(*before, size, -1, *after), dim, 0)


def sent_and_summed(x, axis, dim):
    size = lax.axis_size(axis)
    blocks = lax.all_to_all(cut_along(x, dim, size), axis, 0, 0, tiled=True)
    return jnp.sum(blocks.astype(jnp.float32), axis=0)


def sent_to_all(x, axis):
    copies = jnp.broadcast_to(x, (lax.axis_size(axis), *x.shape))
    return lax.all_to_all(copies, axis, split_axis=0, concat_axis=0, tiled=True)


def laid_out(blocks, dim):
    blocks = jnp.moveaxis(blocks, 0, dim)
    shape = blocks.shape
    return blocks.reshape(*shape[:dim], shape[dim] * shape[dim + 1], *shape[dim + 2 :])


def gathered_copies(x, axis, dim):
    blocks = sent_to_all(x, axis)
    return laid_out(blocks, dim)


def column_info(pair_values, columns):
    boundary = M - pair_values[:, None]
    first_part = columns[None, :] < boundary
    valid_cols = columns[None, :] < M + 1
    second_part = jnp.logical_and(valid_cols, jnp.logical_not(first_part))
    offset = jnp.where(first_part, columns[None, :], columns[None, :] - boundary)
    parity = (1 - 2 * (offset % 2)).astype(jnp.float32)
    degree = jnp.where(first_part, pair_values[:, None] + columns[None, :], columns[None, :] - 1)
    return (
        first_part.astype(jnp.float32),
        second_part.astype(jnp.float32),
        parity,
        degree.astype(jnp.float32),
    )


def wave_numbers(pair_values):
    return jnp.stack([pair_values, M - 1 - pair_values], axis=-1)


def angles(wave_table, positions, length):
    winding = wave_table[..., None] * positions % length
    return winding.astype(jnp.float32) * (2.0 * math.pi / length)


def body(spec, legendre, wave_pairs, row_waves, forcing, helm_coef):
    groups = lax.axis_size("lat")
    lat_id = lax.axis_index("lat")
    lon_id = lax.axis_index("lon")
    fields, _, slot_count, col_width = spec.shape
    half_lats = legendre.shape[2]
    lats_total = 2 * half_lats
    band_rows = row_waves.shape[0]
    seg_width = forcing.shape[2]
    lons_total = seg_width * lax.axis_size("lon")
    my_pairs = lax.dynamic_slice_in_dim(wave_pairs, lat_id * slot_count, slot_count)
    columns = lon_id * col_width + jnp.arange(col_width, dtype=jnp.int32)
    first_part, second_part, parity, degree = column_info(my_pairs, columns)
    selector = jnp.stack([first_part, second_part])
    flip_signs = jnp.stack([jnp.ones_like(parity), parity])
    factor = (selector[:, None] * flip_signs[None]).astype(jnp.bfloat16)
    mixed_terms = factor[:, :, None, None] * spec.astype(jnp.bfloat16)[None, None]
    upward = jnp.einsum(
        "qhfrsc,sck->hkfrsq", mixed_terms, legendre, preferred_element_type=jnp.float32
    ) * (0.5 / math.sqrt(M))
    lat_rows = jnp.concatenate([upward[0], jnp.flip(upward[1], axis=0)], axis=0)
    partial_value = lat_rows.reshape(lats_total, -1).astype(jnp.bfloat16)
    wave_table = wave_numbers(wave_pairs).reshape(groups, slot_count * 2)
    kept_mask = (wave_table[None, :, None, None, :] < row_waves[:, None, None, None, None]).astype(
        jnp.float32
    )
    shares = sent_and_summed(partial_value.astype(jnp.float32).astype(jnp.bfloat16), "lon", 1)
    banded = lax.all_to_all(
        shares.astype(jnp.bfloat16), "lat", split_axis=0, concat_axis=1, tiled=True
    )
    whole = gathered_copies(banded.reshape(band_rows, groups, -1), "lon", 2)
    fourier = whole.reshape(band_rows, groups, fields, 2, slot_count * 2) * kept_mask.astype(
        jnp.bfloat16
    )
    places = lon_id * seg_width + jnp.arange(seg_width, dtype=jnp.int32)
    phases = angles(wave_table, places, lons_total)
    weight = jnp.where(wave_table == 0, 1.0, 2.0).astype(jnp.float32)[..., None]
    forward_table = jnp.stack([weight * jnp.cos(phases), -weight * jnp.sin(phases)]).astype(
        jnp.bfloat16
    )
    grid_field = jnp.einsum(
        "lgfrn,rgnx->flx", fourier, forward_table, preferred_element_type=jnp.float32
    )
    tendency = (forcing - 0.5 * grid_field * grid_field).astype(jnp.bfloat16)
    back_table = (jnp.stack([jnp.cos(phases), -jnp.sin(phases)]) / lons_total).astype(jnp.bfloat16)
    pieces = jnp.einsum("flx,rgnx->lgfrn", tendency, back_table, preferred_element_type=jnp.float32)
    pieces = (pieces * kept_mask).astype(jnp.bfloat16)
    shares_back = sent_and_summed(
        pieces.reshape(band_rows, groups, -1).astype(jnp.float32).astype(jnp.bfloat16), "lon", 2
    )
    swapped = lax.all_to_all(
        shares_back.astype(jnp.bfloat16), "lat", split_axis=1, concat_axis=0, tiled=True
    )
    fan_flat = lax.all_gather(swapped, "lon", axis=2, tiled=True).reshape(lats_total, -1)
    fan_rows = fan_flat.reshape(lats_total, fields, 2, slot_count, 2)
    mixed_back = jnp.stack([fan_rows[:half_lats], jnp.flip(fan_rows[half_lats:], axis=0)])
    downward = jnp.einsum(
        "hkfrsq,sck->frsqhc", mixed_back, legendre, preferred_element_type=jnp.float32
    )
    spectral_tendency = (
        first_part * (downward[:, :, :, 0, 0] + parity * downward[:, :, :, 0, 1])
        + second_part * (downward[:, :, :, 1, 0] + parity * downward[:, :, :, 1, 1])
    ) * math.sqrt(M)
    valid_cols = first_part + second_part
    divisor = 1.0 + helm_coef[:, None, None, None] * (degree * (degree + 1.0))[None, None]
    spec_new = valid_cols[None, None] * (spec + spectral_tendency) / divisor
    return (grid_field, spec_new)


def solution(mesh):
    return jax.shard_map(
        body,
        mesh=mesh,
        in_specs=(
            P(None, None, "lat", "lon"),
            P("lat", "lon", None),
            P(),
            P("lat"),
            P(None, "lat", "lon"),
            P(),
        ),
        out_specs=(P(None, "lat", "lon"), P(None, None, "lat", "lon")),
        check_vma=False,
    )
```

profile of v0, /device:TPU:1, one launch (start us, length us, event | category | flops | bytes accessed | tf_op | source)
XLA Modules:
  0.0 214.0 jit_solution(17737734242475335032)
XLA Ops:
  3.6 4.1 %rev.8 = bf16[1280,4,2,10,2]{0,1,2,4,3:T(4,128)(2,1)} reverse(bf16[1280,4,2,10,2]{0,1,2,4,3:T(4,128)(2,1)S(1)} %get-tuple-element.17), dimensions={0} | reverse | bytes 819200 | tf_op jit(solution)/shard_map/jit(_flip)/rev | solution.py:83
  7.7 2.1 copy.81
  12.0 2.0 concatenate.10
  15.3 51.6 %all_to_all.50 = bf16[16,2560,10]{1,2,0:T(8,128)(2,1)} all-to-all(bf16[16,2560,10]{1,2,0:T(8,128)(2,1)S(1)} %maximum_bitcast_fusion.2), channel_id=1, replica_groups=mesh['lat'=64,'lon'=16] {'lon'}, dimensions={0} | all-to-all | bytes 1638400 | tf_op jit(solution)/shard_map/all_to_all | solution.py:18
  66.9 1.5 reduce_sum.24
  69.1 24.7 %all_to_all.51 = bf16[64,2,200]{2,1,0:T(2,128)(2,1)S(1)} all-to-all(bf16[64,2,200]{2,1,0:T(2,128)(2,1)S(1)} %reshape.638), channel_id=1, replica_groups=mesh['lat'=64,'lon'=16] {'lat'}, dimensions={0} | all-to-all | bytes 102400 | tf_op jit(solution)/shard_map/all_to_all | solution.py:90
  94.2 1.4 broadcast_bitcast_fusion
  95.6 3.9 %reshape.640 = bf16[16,2,12800]{2,1,0:T(2,128)(2,1)} reshape(bf16[16,10,40,64]{3,2,1,0:T(8,128)(2,1)} %broadcast_bitcast_fusion) | data formatting | bytes 1638400
  99.5 4.7 %all-to-all-start.2 = ((bf16[16,2,12800]{2,1,0:T(2,128)(2,1)}), bf16[16,2,12800]{2,1,0:T(2,128)(2,1)S(1)}, u32[]{:S(2)}, u32[]{:S(2)}) async-start(bf16[16,2,12800]{2,1,0:T(2,128)(2,1)} %reshape.640), calls=%async_computation.2 | async-start | bytes 1638400 | tf_op jit(solution)/shard_map/all_to_all | solution.py:24
  105.5 11.0 %fusion.17 = (f32[1,64,20,320]{3,1,0,2:T(8,128)}, bf16[1,64,20,320]{3,1,0,2:T(8,128)(2,1)}, f32[1,64,20,320]{3,1,0,2:T(8,128)}, bf16[1,64,20,320]{3,1,0,2:T(8,128)(2,1)}) fusion(s32[320]{0:T(512)S(1)} %iota_add_fusion, s32[64,20]{0,1:T(8,128)S(1)} %copy.77, f32[64,20]{0,1:T(8,128)S(1)} %get-tuple-element.24, f32[64,20]{0,1:T(8,128)S(1)} %get-tuple-element.25), kind=kLoop, calls=%fused_computation.25 | loop fusion | flops 5734400 | bytes 4931840 | tf_op jit(solution)/shard_map/cos | solution.py:100
  116.5 11.1 %all-to-all-done.2 = bf16[16,2,12800]{2,1,0:T(2,128)(2,1)S(1)} async-done(((bf16[16,2,12800]{2,1,0:T(2,128)(2,1)}), bf16[16,2,12800]{2,1,0:T(2,128)(2,1)S(1)}, u32[]{:S(2)}, u32[]{:S(2)}) %all-to-all-start.2) | async-done | bytes 819232 | tf_op jit(solution)/shard_map/all_to_all | solution.py:24
  127.6 1.9 reshape.641
  129.6 2.9 %fusion.23 = f32[4,40,320]{2,1,0:T(8,128)S(1)} fusion(bf16[1,64,20,320]{3,1,0,2:T(8,128)(2,1)} %get-tuple-element.21, bf16[1,64,20,320]{3,1,0,2:T(8,128)(2,1)} %get-tuple-element.19, bf16[40,64,4,2,20]{1,0,4,3,2:T(8,128)(2,1)} %bitcast.127, bf16[40,64,20]{1,0,2:T(8,128)(2,1)} %get-tuple-element.23), kind=kOutput, calls=%fused_computation.30 | convolution fusion | flops 265830400 | bytes 2764800 | tf_op jit(solution)/shard_map/lgfrn,rgnx->flx/dot_general | solution.py:103
  134.2 1.5 copy.87
  135.7 3.9 %reshape.642 = bf16[16,2,12800]{2,1,0:T(2,128)(2,1)} reshape(bf16[16,10,40,64]{3,2,1,0:T(8,128)(2,1)} %bitcast.126) | data formatting | bytes 1638400
  139.5 3.7 %all-to-all-start.3 = ((bf16[16,2,12800]{2,1,0:T(2,128)(2,1)}), bf16[16,2,12800]{2,1,0:T(2,128)(2,1)S(1)}, u32[]{:S(2)}, u32[]{:S(2)}) async-start(bf16[16,2,12800]{2,1,0:T(2,128)(2,1)} %reshape.642), calls=%async_computation.3 | async-start | bytes 1638400 | tf_op jit(solution)/shard_map/all_to_all | solution.py:18
  143.5 22.5 %all-to-all-done.3 = bf16[16,2,12800]{2,1,0:T(2,128)(2,1)S(1)} async-done(((bf16[16,2,12800]{2,1,0:T(2,128)(2,1)}), bf16[16,2,12800]{2,1,0:T(2,128)(2,1)S(1)}, u32[]{:S(2)}, u32[]{:S(2)}) %all-to-all-start.3) | async-done | bytes 819232 | tf_op jit(solution)/shard_map/all_to_all | solution.py:18
  166.0 2.0 reshape.643
  167.9 1.8 bitcast_reduce_fusion
  170.8 4.6 %all-to-all-start.4 = ((bf16[64,2,200]{2,1,0:T(2,128)(2,1)}), bf16[64,2,200]{2,1,0:T(2,128)(2,1)S(1)}, u32[]{:S(2)}, u32[]{:S(2)}) async-start(bf16[64,2,200]{2,1,0:T(2,128)(2,1)} %reshape.644), calls=%async_computation.4 | async-start | bytes 131072 | tf_op jit(solution)/shard_map/all_to_all | solution.py:113
  175.5 11.0 %all-to-all-done.4 = bf16[64,2,200]{2,1,0:T(2,128)(2,1)S(1)} async-done(((bf16[64,2,200]{2,1,0:T(2,128)(2,1)}), bf16[64,2,200]{2,1,0:T(2,128)(2,1)S(1)}, u32[]{:S(2)}, u32[]{:S(2)}) %all-to-all-start.4) | async-done | bytes 51232 | tf_op jit(solution)/shard_map/all_to_all | solution.py:113
  187.0 19.5 %all_gather.3 = bf16[2560,1,160]{0,1,2:T(2,128)(2,1)S(1)} all-gather(bf16[2560,1,10]{0,1,2:T(2,128)(2,1)S(1)} %all_to_all.44), channel_id=1, replica_groups=mesh['lat'=64,'lon'=16] {'lon'}, dimensions={2}, use_global_device_ids=true | all-gather | bytes 870400 | tf_op jit(solution)/shard_map/all_gather | solution.py:116
  206.5 3.4 %slice_reduce_fusion.1 = (bf16[1280,160]{0,1:T(8,128)(2,1)S(1)}, bf16[1280,160]{0,1:T(8,128)(2,1)S(1)}) fusion(bf16[2560,1,160]{0,1,2:T(2,128)(2,1)S(1)} %all_gather.3), kind=kLoop, calls=%fused_computation.33 | loop fusion | bytes 1638400 | tf_op jit(solution)/shard_map/slice | solution.py:118
  210.3 1.7 rev.9
  (67 shorter events, 14.5 us)
Async XLA Ops:
  0.6 2.0 copy-start
  95.6 8.6 %copy-start.4 = (s32[640]{0:T(1024)S(1)}, s32[640]{0:T(1024)}, u32[]{:S(2)}) copy-start(s32[640]{0:T(1024)} %param.8) | copy-start | bytes 7684
  95.6 9.1 %copy-start.6 = (s32[40]{0:T(128)S(1)}, s32[40]{0:T(128)}, u32[]{:S(2)}) copy-start(s32[40]{0:T(128)} %param.9) | copy-start | bytes 484
  99.5 28.2 %all-to-all-start.2 = ((bf16[16,2,12800]{2,1,0:T(2,128)(2,1)}), bf16[16,2,12800]{2,1,0:T(2,128)(2,1)S(1)}, u32[]{:S(2)}, u32[]{:S(2)}) async-start(bf16[16,2,12800]{2,1,0:T(2,128)(2,1)} %reshape.640), calls=%async_computation.2 | async-start | bytes 1638400 | tf_op jit(solution)/shard_map/all_to_all | solution.py:24
  129.6 2.9 %copy-start.1 = (f32[1,64,20,320]{3,1,0,2:T(8,128)S(1)}, f32[1,64,20,320]{3,1,0,2:T(8,128)}, u32[]{:S(2)}) copy-start(f32[1,64,20,320]{3,1,0,2:T(8,128)} %get-tuple-element.18) | copy-start | bytes 4915204
  129.6 3.3 %copy-start.2 = (f32[1,64,20,320]{3,1,0,2:T(8,128)S(1)}, f32[1,64,20,320]{3,1,0,2:T(8,128)}, u32[]{:S(2)}) copy-start(f32[1,64,20,320]{3,1,0,2:T(8,128)} %get-tuple-element.20) | copy-start | bytes 4915204
  129.6 3.3 %copy-start.7 = (f32[4,40,320]{2,1,0:T(8,128)S(1)}, f32[4,40,320]{2,1,0:T(8,128)}, u32[]{:S(2)}) copy-start(f32[4,40,320]{2,1,0:T(8,128)} %param.10) | copy-start | bytes 614404
  132.5 1.7 copy-start.8
  135.7 7.7 %copy-start.5 = (f32[4]{0:T(128)S(1)}, f32[4]{0:T(128)}, u32[]{:S(2)}) copy-start(f32[4]{0:T(128)} %param.11) | copy-start | bytes 52
  139.5 26.5 %all-to-all-start.3 = ((bf16[16,2,12800]{2,1,0:T(2,128)(2,1)}), bf16[16,2,12800]{2,1,0:T(2,128)(2,1)S(1)}, u32[]{:S(2)}, u32[]{:S(2)}) async-start(bf16[16,2,12800]{2,1,0:T(2,128)(2,1)} %reshape.642), calls=%async_computation.3 | async-start | bytes 1638400 | tf_op jit(solution)/shard_map/all_to_all | solution.py:18
  170.8 15.7 %all-to-all-start.4 = ((bf16[64,2,200]{2,1,0:T(2,128)(2,1)}), bf16[64,2,200]{2,1,0:T(2,128)(2,1)S(1)}, u32[]{:S(2)}, u32[]{:S(2)}) async-start(bf16[64,2,200]{2,1,0:T(2,128)(2,1)} %reshape.644), calls=%async_computation.4 | async-start | bytes 131072 | tf_op jit(solution)/shard_map/all_to_all | solution.py:113
  212.3 1.0 copy-start.3
where the time goes:
time: 215 us; the launch traced here: 214 us
  blocking collectives  95.8 us (45%)
  waiting for transfers between devices  44.6 us (21%)
  local copies, waits for them, and re-layouts  35.1 us (16%)
  other arithmetic  18.7 us (9%)
  starting transfers between devices  13 us (6%)
  matrix products  5.8 us (3%)
    all_to_all x1, blocking collectives, sent_and_summed(): blocks = lax.all_to_all(cut_along(x, dim, size), axis, 0, 0, tiled=True)  51.6 us
    all_to_all x1, blocking collectives, body(): lax.all_to_all(shares.astype(jnp.bfloat16), 'lat', split_axis=0, concat_a...  24.7 us
    all_to_all x1, waiting for transfers between devices, sent_and_summed(): blocks = lax.all_to_all(cut_along(x, dim, size), axis, 0, 0, tiled=True)  22.5 us
    all_gather x1, blocking collectives, body(): lax.all_gather(swapped, 'lon', axis=2, tiled=True).reshape(lats_total, -1)  19.5 us
    unnamed x28, local copies, waits for them, and re-layouts  15.6 us
    all_to_all x1, waiting for transfers between devices, sent_to_all(): return lax.all_to_all(copies, axis, split_axis=0, concat_axis=0, tiled=True)  11.1 us
    cos x1, other arithmetic, body(): jnp.cos(phases)  11 us
    all_to_all x1, waiting for transfers between devices, body(): lax.all_to_all(shares_back.astype(jnp.bfloat16), 'lat', split_axis=1, con...  11 us
  transfers between devices with their start and end apart: 3, of which 3 were waited for; matrix products, arithmetic and copies ran while one was open for 6% of the time, Pallas kernels for 0%

commit v1 on v0

v1 whole, which is shorter than its diff:
```python
import math

import jax
import jax.numpy as jnp
import numpy as np
from jax import lax
from jax.experimental import pallas as pl
from jax.experimental.pallas import tpu as pltpu
from jax.sharding import PartitionSpec as P

M = 1280
NLON = 5120
SEG = 320
MESH = pl.DeviceIdType.MESH
F32, BF16, I32 = jnp.float32, jnp.bfloat16, jnp.int32


def tables():
    x = np.arange(SEG)
    a = np.arange(40)
    psi = 2 * np.pi * ((a[None, :] * x[:, None]) % SEG) / SEG
    cos_ax, sin_ax = np.cos(psi), np.sin(psi)

    def alpha(b, q):
        m = np.where(q == 0, b, M - 1 - b)
        return 2 * np.pi * ((m[None, :] * x[:, None]) % NLON) / NLON

    t2rep = np.zeros((640, 256))
    t2rep[:, :240] = np.tile(np.concatenate([cos_ax, sin_ax]), (1, 6))
    lane = np.arange(240)
    b6, r, i, q = lane // 40, lane % 40 // 20, lane % 20 // 2, lane % 2
    twa, twb = np.zeros((3, SEG, 256)), np.zeros((3, SEG, 256))
    w1, w2 = np.zeros((3, 240, 256)), np.zeros((3, 240, 256))
    col = np.arange(256)
    d, icol = col // 16, col % 16
    for g in range(3):
        b = 6 * g + b6
        ok = b < 16
        twa[g, :, :240] = np.cos(alpha(b, q)) * ok
        twb[g, :, :240] = np.sin(alpha(b, q)) * ok
        bq = np.where(q == 0, b, 15 - b)
        beta = 2 * np.pi * ((bq[:, None] * d[None, :]) % 16) / 16
        same = (i[:, None] == icol[None, :]) * ok[:, None] * 2.0
        w1[g] = same * np.where(r[:, None] == 0, np.cos(beta), -np.sin(beta))
        w2[g] = same * np.where(r[:, None] == 0, -np.sin(beta), -np.cos(beta))
    rep = np.zeros((3, 128, 256))
    for s3 in range(3):
        rep[s3, 40 * s3 + lane % 40, lane] = 1.0
    ca = np.concatenate([t2rep, *twa, *twb, *w1, *w2, *rep])
    lane = np.arange(512)
    b, i, q = lane // 32, lane % 32 // 2, lane % 2
    ok = lane % 32 < 20
    bq = np.where(q == 0, b, 15 - b)
    beta = 2 * np.pi * ((bq[None, :] * d[:, None]) % 16) / 16
    same = (i[None, :] == icol[:, None]) * ok[None, :] * 1.0
    cb = np.concatenate(
        [same * np.cos(beta), -same * np.sin(beta), np.cos(alpha(b, q)) * ok, np.sin(alpha(b, q)) * ok]
    )
    cc = np.concatenate([cos_ax.T, sin_ax.T])
    svec = np.full((2, 16, 512), -1, np.int32)
    s2vec = np.full((2, 8, M), -1, np.int32)
    for core in range(2):
        for i in range(10):
            line = i if core == 0 else 9 - i
            for rho in range(40):
                s, r, q = rho // 4, rho % 4 // 2, rho % 2
                target = s // 3 * 128 + s % 3 * 40 + r * 20 + line * 2 + q
                svec[core, i, target] = rho
                s2vec[core, :, i * 128 + rho] = target
    return [jnp.asarray(t, BF16) for t in (ca, cb, cc)] + [jnp.asarray(svec), jnp.asarray(s2vec)]


T2, TWA, TWB, W1, W2, REP = 0, 640, 1600, 2560, 3280, 4000


def band_of(lat, half, hemi):
    z, y = lat // 8, lat % 8
    even = jnp.where(hemi == 0, 2 * half, 6 - 2 * half)
    delta = (z - even + 8) % 8
    near = jnp.logical_and(delta >= 1, delta <= 4)
    band = jnp.where(near, even + 1, even) * 8 + y
    quarter = jnp.where(near, delta - 1, (8 - delta) % 8)
    return band, quarter


def block_of(lat, half, hemi):
    band, quarter = band_of(lat, half, hemi)
    north = jnp.where(hemi == 0, band, 63 - band)
    return 4 * (north - 16 * half) + jnp.where(hemi == 0, quarter, 3 - quarter)


def owner_of(band, quarter, field):
    hemi = band // 32
    north = jnp.where(hemi == 0, band, 63 - band)
    z, y = band // 8, band % 8
    z = (z + jnp.where(z % 2 == 1, quarter, 8 - quarter)) % 8
    return z * 8 + y, 2 * (4 * (north // 16) + field) + hemi


def iota(shape, dim):
    return lax.broadcasted_iota(I32, shape, dim)


def dot(x, y):
    return jnp.dot(x, y, preferred_element_type=F32)


def kernel(
    mix, leg, fsend, rwx, wrow, wcol, ca, cb, cc, svec, s2vec, fac, sel, spec_t, mul_t,
    grid_out, spec_out,
    cav, cbv, ccv, part, prcv, summ, xrcv, xt, tt, smat, s2m, oht, oh, bbuf, brcv, frcv, rwrcv,
    bd, gbuf, grcv, abuf, ebuf, ercv, fall,
    csem, psem, fs, fr, xs, xr, bs, br, es, er, gs, gr, as_, ar, ws, wr,
):
    lat, lon = lax.axis_index("lat"), lax.axis_index("lon")
    chip, core = lon // 2, lon % 2
    half, field = chip // 4, chip % 4
    partner = 2 * chip + 1 - core
    band, quarter = band_of(lat, half, core)

    barrier = pltpu.get_barrier_semaphore()

    def greet(to_lat, to_lon):
        pl.semaphore_signal(barrier, inc=1, device_id=(to_lat, to_lon), device_id_type=MESH)

    greet(lat, partner)

    @pl.loop(1, 8)
    def _(t):
        greet(lat, 2 * ((chip + t) % 8) + core)

    @pl.loop(0, 16)
    def _(n):
        to_lat, to_lon = owner_of(lat, n // 4, n % 4)

        @pl.when(jnp.logical_or(to_lat != lat, to_lon != lon))
        def _():
            greet(to_lat, to_lon)

        @pl.when(jnp.logical_or(band != lat, n != lon))
        def _():
            greet(band, n)

    @pl.loop(1, 64)
    def _(t):
        greet((lat + t) % 64, lon)

    consts = [
        pltpu.make_async_copy(src, dst, csem.at[n])
        for n, (src, dst) in enumerate([(ca, cav), (cb, cbv), (cc, ccv)])
    ]
    for copy in consts:
        copy.start()

    @pl.loop(0, 5)
    def _(sp):
        terms = dot(mix[2 * sp], leg[2 * sp]) + dot(mix[2 * sp + 1], leg[2 * sp + 1])
        terms = (terms * (0.5 / math.sqrt(M))).astype(BF16)
        part[:, :, sp] = terms.reshape(2, 4, 8, M)

    my_slot_lat, my_slot_lon = owner_of(lat, 0, field)
    is_self = jnp.logical_and(my_slot_lat == lat, my_slot_lon == lon)
    pl.semaphore_wait(barrier, 103 - 2 * is_self.astype(I32))

    swap = pltpu.make_async_remote_copy(
        part.at[1 - core], prcv, psem.at[0], psem.at[1], device_id=(lat, partner), device_id_type=MESH
    )
    swap.start()

    def forcing_copy(n):
        to_lat, to_lon = owner_of(lat, n // 4, n % 4)
        away = jnp.logical_or(to_lat != lat, to_lon != lon)
        src, dst = fsend.at[n % 4, n // 4], frcv.at[lon]
        remote = pltpu.make_async_remote_copy(
            src, dst, fs.at[n], fr.at[0], device_id=(to_lat, to_lon), device_id_type=MESH
        )
        return away, remote, pltpu.make_async_copy(src, dst, fr.at[0])

    def rows_copy():
        to_lat, to_lon = owner_of(lat, lon // 4, lon % 4)
        away = jnp.logical_or(to_lat != lat, to_lon != lon)
        remote = pltpu.make_async_remote_copy(
            rwx.at[lon // 4], rwrcv, ws, wr, device_id=(to_lat, to_lon), device_id_type=MESH
        )
        return away, remote, pltpu.make_async_copy(rwx.at[lon // 4], rwrcv, wr)

    def launch(away, remote, local):
        @pl.when(away)
        def _():
            remote.start()

        @pl.when(jnp.logical_not(away))
        def _():
            local.start()

    swap.wait_recv()
    summ[...] = (part[core].astype(F32) + prcv[...].astype(F32)).astype(BF16)

    def shared(which, to):
        return pltpu.make_async_remote_copy(
            summ.at[to % 4, :, :, pl.ds(pl.multiple_of(640 * (to // 4), 128), 640)],
            xrcv.at[which], xs.at[which], xr.at[which], device_id=(lat, 2 * to + core), device_id_type=MESH,
        )

    for t in (4, 3, 5, 2, 6, 1, 7):
        shared(t, (chip + t) % 8).start()

    @pl.loop(0, 16)
    def _(n):
        launch(*forcing_copy(n))

    launch(*rows_copy())

    lanes = iota((128, 512), 0)
    for i in range(10):
        smat[i] = (svec[core, i : i + 1, :] == lanes).astype(BF16)
    for s3 in range(3):
        oht[s3] = (wrow[s3, 0:1, :] == iota((640, 256), 0)).astype(BF16)
    for t in range(5):
        oh[:, 128 * t : 128 * t + 128] = (wcol[...] == iota((768, 128), 1) + 128 * t).astype(BF16)
    s2m[...] = (s2vec[core, 0:1, :] == iota((512, M), 0)).astype(BF16)

    total = summ[field, :, :, pl.ds(pl.multiple_of(640 * half, 128), 640)].astype(F32)
    for t in (1, 7, 2, 6, 3, 5, 4):
        shared(t, (chip + t) % 8).wait_recv()
        total = total + xrcv[t].astype(F32)
    xt[0:40, :] = total.reshape(40, 640)
    xt[40:128, :] = jnp.zeros((88, 640), F32)
    tt[...] = xt[...].T
    packed = dot(tt[pl.ds(0, 64, stride=10), :].astype(BF16), smat[0])
    for i in range(1, 10):
        packed += dot(tt[pl.ds(i, 64, stride=10), :].astype(BF16), smat[i])
    for j in range(4):
        bbuf[:, j, :] = packed[:, 128 * j : 128 * j + 128]

    def to_lines(t):
        to = (lat + t) % 64
        return pltpu.make_async_remote_copy(
            bbuf.at[block_of(to, half, core)], brcv.at[lat], bs, br, device_id=(to, lon), device_id_type=MESH
        )

    @pl.loop(1, 64)
    def _(t):
        to_lines(t).start()

    pltpu.make_async_copy(bbuf.at[block_of(lat, half, core)], brcv.at[lat], br).start()
    pltpu.make_async_copy(frcv, frcv, fr.at[0]).wait()
    push = frcv[...].astype(F32).reshape(256, SEG).T
    pltpu.make_async_copy(rwrcv, rwrcv, wr).wait()
    for copy in consts:
        copy.wait()
    pltpu.make_async_copy(brcv, brcv, br).wait()

    rows = jnp.concatenate([brcv[:, j, :].astype(BF16) for j in range(4)], axis=0)
    coef = jnp.zeros((640, 240), F32)
    for s3 in range(3):
        spread = dot(rows, cav[REP + 128 * s3 : REP + 128 * s3 + 128, :240]).astype(BF16)
        coef += dot(oht[s3], spread)
    lane = iota((40, 240), 1)
    for b in range(16):
        m = iota((40, 240), 0) * 16 + b
        m = jnp.where(lane % 2 == 1, M - 1 - m, m)
        low = 40 * (b % 6)
        keep = jnp.logical_and(lane >= low, lane < low + 40)
        keep = jnp.logical_and(keep, m.astype(F32) < rwrcv[0:1, 0:240])
        value = jnp.where(keep, coef[40 * b : 40 * b + 40], 0.0)
        if b == 0:
            value = jnp.where(m == 0, 0.5 * value, value)
        bd[40 * b : 40 * b + 40, :] = value.astype(BF16)

    sign = jnp.where(iota((1, 240), 1) % 2 == 1, -1.0, 1.0)
    y = jnp.zeros((SEG, 256), F32)
    for g, depth in enumerate((240, 240, 160)):
        cs = dot(cav[T2 : T2 + 640, :depth], bd[240 * g : 240 * g + depth, :])
        c, s = cs[:SEG], cs[SEG:] * sign
        ta = cav[TWA + SEG * g : TWA + SEG * g + SEG, :240].astype(F32)
        tb = cav[TWB + SEG * g : TWB + SEG * g + SEG, :240].astype(F32)
        y += dot((ta * c - tb * s).astype(BF16), cav[W1 + 240 * g : W1 + 240 * g + 240, :])
        y += dot((tb * c + ta * s).astype(BF16), cav[W2 + 240 * g : W2 + 240 * g + 240, :])
    tend = (push - 0.5 * y * y).astype(BF16)
    gbuf[...] = y.T.astype(BF16).reshape(16, 16, SEG)

    gc, gi = dot(tend, cbv[0:256, :]), dot(tend, cbv[256:512, :])
    ta, tb = cbv[512:832, :].astype(F32), cbv[832:1152, :].astype(F32)
    kc = dot(ccv[...], (ta * gc + tb * gi).astype(BF16))
    ks = dot(ccv[...], (ta * gi - tb * gc).astype(BF16))
    lane = iota((40, 512), 1)
    sign = jnp.where(lane % 2 == 1, -1.0, 1.0)
    m = iota((40, 512), 0) * 16 + lane // 32
    m = jnp.where(lane % 2 == 1, M - 1 - m, m)
    scale = jnp.where(m.astype(F32) < rwrcv[0:1, 256:768], 1.0 / NLON, 0.0)
    real = (kc[:40] + sign * ks[40:]) * scale
    imag = (ks[:40] - sign * kc[40:]) * scale
    lane = iota((40, 128), 1)
    for b in range(16):
        tile, off = 128 * (b // 4), 32 * (b % 4)
        re, im = real[:, tile : tile + 128], imag[:, tile : tile + 128]
        re = pltpu.roll(re, (128 - off) % 128, 1) if off else re
        im = pltpu.roll(im, (148 - off) % 128, 1)
        value = jnp.where(lane < 20, re, jnp.where(lane < 40, im, 0.0))
        abuf[0, 40 * b : 40 * b + 40, :] = value.astype(BF16)
        abuf[1, 40 * b : 40 * b + 40, :] = pltpu.roll(value, 40, 1).astype(BF16)
        abuf[2, 40 * b : 40 * b + 40, :] = pltpu.roll(value, 80, 1).astype(BF16)
    back = jnp.zeros((256, 128), F32)
    for s3 in range(3):
        back += dot(oh[256 * s3 : 256 * s3 + 256, :], abuf[s3])
    for j in range(4):
        ebuf[:, j, :] = back[64 * j : 64 * j + 64]

    block = block_of(lat, half, core)

    def to_waves(t):
        to = (lat + t) % 64
        return pltpu.make_async_remote_copy(
            ebuf.at[to], ercv.at[block], es, er, device_id=(to, lon), device_id_type=MESH
        )

    @pl.loop(1, 64)
    def _(t):
        to_waves(t).start()

    pltpu.make_async_copy(ebuf.at[lat], ercv.at[block], er).start()

    def grid_copy(n):
        away = jnp.logical_or(band != lat, n != lon)
        src, dst = gbuf.at[n], grcv.at[field, quarter]
        remote = pltpu.make_async_remote_copy(
            src, dst, gs.at[n], gr, device_id=(band, n), device_id_type=MESH
        )
        return away, remote, pltpu.make_async_copy(src, dst, gr)

    @pl.loop(0, 16)
    def _(n):
        launch(*grid_copy(n))

    pltpu.make_async_copy(ercv, ercv, er).wait()
    rows = jnp.concatenate([ercv[:, j, :].astype(BF16) for j in range(4)], axis=1)
    placed = dot(rows, s2m[...])
    for i in range(10):
        tt[pl.ds(i, 64, stride=10), :] = placed[:, 128 * i : 128 * i + 128]
    xt[...] = tt[...].T
    fall[core, chip] = xt[0:40, :].astype(BF16).reshape(5, 8, 640)

    def around(t):
        to = (chip + t) % 8
        return pltpu.make_async_remote_copy(
            fall.at[core, chip], fall.at[core, chip], as_.at[t], ar.at[t],
            device_id=(lat, 2 * to + core), device_id_type=MESH,
        )

    def across(t):
        which = (chip + 8 - t) % 8
        return pltpu.make_async_remote_copy(
            fall.at[core, which], fall.at[core, which], as_.at[8 + t], ar.at[8 + t],
            device_id=(lat, partner), device_id_type=MESH,
        )

    for t in (4, 3, 5, 2, 6, 1, 7):
        around(t).start()
    across(0).start()
    for t in (1, 7, 2, 6, 3, 5, 4):
        pltpu.make_async_copy(fall.at[core, 0], fall.at[core, 0], ar.at[t]).wait()
        across(t).start()
    for t in range(8):
        across(t).wait_recv()

    nt = (((1,), (1,)), ((), ()))

    @pl.loop(0, 5)
    def _(sp):
        lows, highs = fall[:, 0:4, sp], fall[:, 4:8, sp]
        low = lows.astype(F32).reshape(64, 640).astype(BF16)
        high = highs.astype(F32).reshape(64, 640).astype(BF16)
        for s2 in range(2):
            basis = leg[2 * sp + s2]
            sums = lax.dot_general(low, basis[:, :640], nt, preferred_element_type=F32)
            sums += lax.dot_general(high, basis[:, 640:], nt, preferred_element_type=F32)
            sums = sums * fac[2 * sp + s2]
            folded = jnp.dot(sel[...], sums, preferred_element_type=F32, precision=lax.Precision.HIGHEST)
            spec_out[2 * sp + s2] = (spec_t[2 * sp + s2] + folded) * mul_t[2 * sp + s2]

    pltpu.make_async_copy(grcv, grcv, gr).wait()
    for f in range(4):
        for w in range(4):
            grid_out[f, 10 * w : 10 * w + 10, :] = grcv[f, w].astype(F32)[:10]

    swap.wait_send()
    for t in range(1, 8):
        shared(t, (chip + t) % 8).wait_send()
        around(t).wait_send()
    for t in range(8):
        across(t).wait_send()
    rest = brcv.at[pl.ds(0, 63)]
    pltpu.make_async_copy(rest, rest, bs).wait()
    pltpu.make_async_copy(rest, rest, es).wait()

    @pl.loop(0, 16)
    def _(n):
        away, remote, _ = forcing_copy(n)

        @pl.when(away)
        def _():
            remote.wait_send()

        away, remote, _ = grid_copy(n)

        @pl.when(away)
        def _():
            remote.wait_send()

    away, remote, _ = rows_copy()

    @pl.when(away)
    def _():
        remote.wait_send()


def body(spec, legendre, wave_pairs, row_waves, forcing, helm_coef):
    lat_id, lon_id = lax.axis_index("lat"), lax.axis_index("lon")
    v = lax.dynamic_slice_in_dim(wave_pairs, lat_id * 10, 10)[:, None]
    col = (lon_id * 84 + jnp.arange(84, dtype=I32))[None, :]
    edge = M - v
    first = col < edge
    valid = col < M + 1
    second = jnp.logical_and(valid, jnp.logical_not(first))
    offset = jnp.where(first, col, col - edge)
    parity = (1 - 2 * (offset % 2)).astype(F32)
    degree = jnp.where(first, v + col, col - 1).astype(F32)

    parts = jnp.stack([first, second], axis=1).astype(F32)[:, None, None, None, None]
    signs = jnp.stack([jnp.ones_like(parity), parity], axis=1)[:, :, None, None, None, None]
    slot = (jnp.arange(10)[:, None] % 2 == jnp.arange(2)[None, :]).astype(F32)
    factor = parts * signs * slot[:, None, None, :, None, None, None]
    spec_t = jnp.transpose(spec, (2, 0, 1, 3))
    mix = factor * spec_t.astype(BF16).astype(F32)[:, None, :, None, :, None]
    mix = mix.astype(BF16).reshape(10, 64, 84)
    fac = jnp.broadcast_to(factor * math.sqrt(M), (10, 2, 4, 2, 2, 2, 84)).reshape(10, 64, 84)
    row = np.arange(64)
    sel = jnp.asarray((row[None, :] // 8 % 4 * 2 + row[None, :] // 2 % 2) == np.arange(8)[:, None], F32)
    divisor = 1.0 + helm_coef[None, :, None] * (degree * (degree + 1.0))[:, None, :]
    mul_t = valid.astype(F32)[:, None, :] / divisor
    mul_t = jnp.broadcast_to(mul_t[:, :, None], (10, 4, 2, 84)).reshape(10, 8, 84)

    fsend = forcing.astype(BF16).reshape(4, 4, 10, SEG)
    fsend = jnp.pad(fsend, ((0, 0), (0, 0), (0, 6), (0, 0)))
    limits = jnp.repeat(row_waves.astype(F32).reshape(4, 10), 2, axis=1)
    rwx = jnp.concatenate(
        [
            jnp.pad(jnp.tile(limits, (1, 12)), ((0, 0), (0, 16))),
            jnp.tile(jnp.pad(limits, ((0, 0), (0, 12))), (1, 16)),
        ],
        axis=1,
    )
    rwx = jnp.broadcast_to(rwx[:, None], (4, 8, 768))
    place = (wave_pairs % 16 * 40 + wave_pairs // 16).reshape(64, 10)
    place = jnp.pad(place, ((0, 0), (0, 2)), constant_values=-1).reshape(64, 4, 3)
    place = jnp.transpose(place, (2, 1, 0)).reshape(3, 256)
    wrow = jnp.broadcast_to(place[:, None], (3, 8, 256))
    wcol = jnp.broadcast_to(place.reshape(768, 1), (768, 128))

    ca, cb, cc, svec, s2vec = tables()
    vmem, hbm = pl.BlockSpec(memory_space=pltpu.VMEM), pl.BlockSpec(memory_space=pl.ANY)
    dma = pltpu.SemaphoreType.DMA
    grid_field, spec_new = pl.pallas_call(
        kernel,
        out_shape=(
            jax.ShapeDtypeStruct((4, 40, SEG), F32),
            jax.ShapeDtypeStruct((10, 8, 84), F32),
        ),
        in_specs=[vmem] * 6 + [hbm] * 3 + [vmem] * 6,
        out_specs=(vmem, vmem),
        scratch_shapes=[
            pltpu.VMEM((4384, 256), BF16), pltpu.VMEM((1152, 512), BF16), pltpu.VMEM((80, SEG), BF16),
            pltpu.VMEM((2, 4, 5, 8, M), BF16), pltpu.VMEM((4, 5, 8, M), BF16), pltpu.VMEM((4, 5, 8, M), BF16),
            pltpu.VMEM((8, 5, 8, 640), BF16), pltpu.VMEM((128, 640), F32), pltpu.VMEM((640, 128), F32),
            pltpu.VMEM((10, 128, 512), BF16), pltpu.VMEM((512, M), BF16), pltpu.VMEM((3, 640, 256), BF16),
            pltpu.VMEM((768, 640), BF16), pltpu.VMEM((64, 4, 128), F32), pltpu.VMEM((64, 4, 128), F32),
            pltpu.VMEM((16, 16, SEG), BF16), pltpu.VMEM((8, 768), F32), pltpu.VMEM((640, 240), BF16),
            pltpu.VMEM((16, 16, SEG), BF16), pltpu.VMEM((4, 4, 16, SEG), BF16), pltpu.VMEM((3, 640, 128), BF16),
            pltpu.VMEM((64, 4, 128), F32), pltpu.VMEM((64, 4, 128), F32), pltpu.VMEM((2, 8, 5, 8, 640), BF16),
            dma((3,)), dma((2,)), dma((16,)), dma((1,)), dma((8,)), dma((8,)), dma, dma, dma, dma,
            dma((16,)), dma, dma((16,)), dma((16,)), dma, dma,
        ],
        compiler_params=pltpu.CompilerParams(
            collective_id=0, has_side_effects=True, vmem_limit_bytes=60 * 1024 * 1024
        ),
        name="step",
    )(mix, legendre, fsend, rwx, wrow, wcol, ca, cb, cc, svec, s2vec, fac, sel, spec_t.reshape(10, 8, 84), mul_t)
    spec_new = jnp.transpose(spec_new.reshape(10, 4, 2, 84), (1, 2, 0, 3))
    return (grid_field, spec_new)


def solution(mesh):
    return jax.shard_map(
        body,
        mesh=mesh,
        in_specs=(
            P(None, None, "lat", "lon"),
            P("lat", "lon", None),
            P(),
            P("lat"),
            P(None, "lat", "lon"),
            P(),
        ),
        out_specs=(P(None, "lat", "lon"), P(None, None, "lat", "lon")),
        check_vma=False,
    )
```

time: 215 us -> 96.6 us (0.45)
  blocking collectives: 95.8 us -> 0 us
  Pallas kernels: 0 us -> 80.5 us
  waiting for transfers between devices: 44.6 us -> 0 us
  local copies, waits for them, and re-layouts: 35.1 us -> 9.74 us
  other arithmetic: 18.7 us -> 5.1 us
  starting transfers between devices: 13 us -> 0 us
  matrix products: 5.8 us -> 0 us
    pallas_call x0 -> x1, Pallas kernels: none -> 80.5 us  [body(): pl.pallas_call(kernel, out_shape=(jax.ShapeDtypeStruct((4, 40, SEG), F32)...]
    all_to_all x2 -> x0, blocking collectives: 76.3 us -> none  [the longest x1 51.6 us: sent_and_summed(): blocks = lax.all_to_all(cut_along(x, dim, size), axis, 0, 0, tiled=True)]
    all_to_all x3 -> x0, waiting for transfers between devices: 44.6 us -> none  [the longest x1 22.5 us: sent_and_summed(): blocks = lax.all_to_all(cut_along(x, dim, size), axis, 0, 0, tiled=True)]
    all_gather x1 -> x0, blocking collectives: 19.5 us -> none  [body(): lax.all_gather(swapped, 'lon', axis=2, tiled=True).reshape(lats_total, -1)]
    unnamed x28 -> x4, local copies, waits for them, and re-layouts: 15.6 us -> 1.73 us
    all_to_all x3 -> x0, starting transfers between devices: 13 us -> none  [the longest x1 4.73 us: sent_to_all(): return lax.all_to_all(copies, axis, split_axis=0, concat_axis=0, tiled=True)]
    cos x1 -> x0, other arithmetic: 11 us -> none  [body(): jnp.cos(phases)]
    dot_general x4 -> x0, matrix products: 5.8 us -> none  [the longest x1 2.9 us: body(): jnp.einsum('lgfrn,rgnx->flx', fourier, forward_table, preferred_element_t...]
  transfers between devices with their start and end apart: 3 -> 0, of which waited for: 3 -> 0; matrix products, arithmetic and copies ran while one was open for 6% -> 0% of each run, Pallas kernels for 0% -> 0%
where the time goes in v1:
time: 96.6 us; the launch traced here: 96.1 us
  Pallas kernels  80.5 us (83%)
  local copies, waits for them, and re-layouts  9.74 us (10%)
  other arithmetic  5.1 us (5%)
    pallas_call x1, Pallas kernels, body(): pl.pallas_call(kernel, out_shape=(jax.ShapeDtypeStruct((4, 40, SEG), F32)...  80.5 us

profile of v1, /device:TPU:1, one launch (start us, length us, event | category | flops | bytes accessed | tf_op | source)
XLA Modules:
  0.0 96.1 jit_solution(3711423258102752936)
XLA Ops:
  0.6 0.7 convert_element_type.73
  1.3 0.8 broadcast_subtract_fusion
  2.1 0.1 reshape.433
  2.2 0.7 fusion.6
  2.9 0.1 fusion.3
  3.0 0.1 copy.32
  3.1 0.1 copy.33
  3.5 0.7 add_divide_fusion
  4.2 0.6 broadcast_in_dim.38
  4.9 0.1 reshape.434
  5.3 0.6 broadcast_in_dim.33.wrow
  5.9 0.1 tile.21
  6.0 0.1 tile.23
  6.1 1.4 %copy.38 = f32[10,4,2,84]{3,2,1,0:T(2,128)} copy(f32[10,4,2,84]{3,2,0,1:T(2,128)} %bitcast.23) | data formatting | bytes 53760 | tf_op jit(solution)/shard_map/transpose | solution.py:434
  7.5 0.1 broadcast_multiply_fusion
  7.6 0.6 broadcast_in_dim.31.rwx
  8.2 1.0 convert_element_type.72
  9.3 0.7 pad.17.fsend
  10.0 0.8 multiply_convert_fusion
  10.8 0.8 broadcast_in_dim.36
  11.6 0.9 broadcast_in_dim.35.wcol
  12.5 80.5 %step.1 = (f32[4,40,320]{2,1,0:T(8,128)}, f32[10,8,84]{2,1,0:T(8,128)}) custom-call(bf16[10,64,84]{2,1,0:T(8,128)(2,1)} %bitcast.19, bf16[10,84,1280]{2,1,0:T(8,128)(2,1)} %leg.1, bf16[4,4,16,320]{3,2,1,0:T(8,128)(2,1)} %pad.17.fsend, f32[4,8,768]{2,1,0:T(8,128)} %broadcast_in_dim.31.rwx, s32[3,8,256]{2,1,0:T(8,128)} %broadcast_in_dim.33.wrow, ...), custom_call_target="tpu_custom_call" | custom-call | tf_op jit(solution)/shard_map/step/pallas_call | solution.py:464
  93.1 1.4 %copy.45 = f32[10,4,2,84]{3,2,0,1:T(2,128)} copy(f32[10,4,2,84]{3,2,1,0:T(2,128)} %bitcast.24) | data formatting | bytes 53760 | tf_op jit(solution)/shard_map/reshape | solution.py:489
  94.5 1.7 %copy.47 = f32[4,40,320]{2,1,0:T(8,128)} copy(f32[4,40,320]{2,1,0:T(8,128)} %get-tuple-element.18) | data formatting | bytes 409600
  (25 shorter events, 0.7 us)
Async XLA Ops:
  0.6 9.4 %copy-start = (f32[4,2,10,84]{3,1,2,0:T(2,128)S(1)}, f32[4,2,10,84]{3,1,2,0:T(2,128)}, u32[]{:S(2)}) copy-start(f32[4,2,10,84]{3,1,2,0:T(2,128)} %param.12) | copy-start | bytes 80644

commit v2 on v1

v2 whole, which is shorter than its diff:
```python
import math

import jax
import jax.numpy as jnp
import numpy as np
from jax import lax
from jax.experimental import pallas as pl
from jax.experimental.pallas import tpu as pltpu
from jax.sharding import PartitionSpec as P

M = 1280
NLON = 5120
SEG = 320
MESH = pl.DeviceIdType.MESH
F32, BF16, I32 = jnp.float32, jnp.bfloat16, jnp.int32


def tables():
    x = np.arange(SEG)
    a = np.arange(40)
    psi = 2 * np.pi * ((a[None, :] * x[:, None]) % SEG) / SEG
    cos_ax, sin_ax = np.cos(psi), np.sin(psi)

    def alpha(b, q):
        m = np.where(q == 0, b, M - 1 - b)
        return 2 * np.pi * ((m[None, :] * x[:, None]) % NLON) / NLON

    t2rep = np.zeros((640, 256))
    t2rep[:, :240] = np.tile(np.concatenate([cos_ax, sin_ax]), (1, 6))
    base = np.zeros((640, 256))
    slot = np.arange(32)
    base[:, :32] = np.concatenate([np.cos(alpha(slot // 2, slot % 2)), np.sin(alpha(slot // 2, slot % 2))])
    lane = np.arange(240)
    b6, r, i, q = lane // 40, lane % 40 // 20, lane % 20 // 2, lane % 2
    w1, w2 = np.zeros((3, 240, 256)), np.zeros((3, 240, 256))
    col = np.arange(256)
    d, icol = col // 16, col % 16
    vecs = np.full((8, M), -1, np.int32)
    for g in range(3):
        b = 6 * g + b6
        ok = b < 16
        vecs[0, 256 * g : 256 * g + 240] = np.where(ok, 2 * b + q, -1)
        bq = np.where(q == 0, b, 15 - b)
        beta = 2 * np.pi * ((bq[:, None] * d[None, :]) % 16) / 16
        same = (i[:, None] == icol[None, :]) * ok[:, None] * 2.0
        w1[g] = same * np.where(r[:, None] == 0, np.cos(beta), -np.sin(beta))
        w2[g] = same * np.where(r[:, None] == 0, -np.sin(beta), -np.cos(beta))
    rep = np.zeros((3, 128, 256))
    for s3 in range(3):
        rep[s3, 40 * s3 + lane % 40, lane] = 1.0
    ca = np.concatenate([t2rep, base, *w1, *w2, *rep])
    vecs[2, :240] = i
    vecs[2, 240:768] = -1000
    lane = np.arange(512)
    b, i, q = lane // 32, lane % 32 // 2, lane % 2
    ok = lane % 32 < 20
    vecs[0, 768:] = np.where(ok, 2 * b + q, -1)
    vecs[2, 256:768] = np.where(ok, i, -1000)
    bq = np.where(q == 0, b, 15 - b)
    beta = 2 * np.pi * ((bq[None, :] * d[:, None]) % 16) / 16
    same = (i[None, :] == icol[:, None]) * ok[None, :] * 1.0
    cb = np.concatenate([same * np.cos(beta), -same * np.sin(beta)])
    cc = np.concatenate([cos_ax.T, sin_ax.T])
    lane = np.arange(768)
    s = 3 * (lane % 256 // 64) + lane // 256
    vecs[1, :768] = np.where(s < 10, 10 * (lane % 64) + s, -1)
    svec = np.full((2, 16, 512), -1, np.int32)
    s2vec = np.full((2, 8, M), -1, np.int32)
    for core in range(2):
        for i in range(10):
            line = i if core == 0 else 9 - i
            for rho in range(40):
                s, r, q = rho // 4, rho % 4 // 2, rho % 2
                target = s // 3 * 128 + s % 3 * 40 + r * 20 + line * 2 + q
                svec[core, i, target] = rho
                s2vec[core, :, i * 128 + rho] = target
    return [jnp.asarray(t, BF16) for t in (ca, cb, cc)] + [jnp.asarray(t) for t in (svec, s2vec, vecs)]


T2, BASE, W1, W2, REP = 0, 640, 1280, 2000, 2720


def band_of(lat, half, hemi):
    z, y = lat // 8, lat % 8
    even = jnp.where(hemi == 0, 2 * half, 6 - 2 * half)
    delta = (z - even + 8) % 8
    near = jnp.logical_and(delta >= 1, delta <= 4)
    band = jnp.where(near, even + 1, even) * 8 + y
    quarter = jnp.where(near, delta - 1, (8 - delta) % 8)
    return band, quarter


def block_of(lat, half, hemi):
    band, quarter = band_of(lat, half, hemi)
    north = jnp.where(hemi == 0, band, 63 - band)
    return 4 * (north - 16 * half) + jnp.where(hemi == 0, quarter, 3 - quarter)


def owner_of(band, quarter, field):
    hemi = band // 32
    north = jnp.where(hemi == 0, band, 63 - band)
    z, y = band // 8, band % 8
    z = (z + jnp.where(z % 2 == 1, quarter, 8 - quarter)) % 8
    return z * 8 + y, 2 * (4 * (north // 16) + field) + hemi


def iota(shape, dim):
    return lax.broadcasted_iota(I32, shape, dim)


def dot(x, y):
    return jnp.dot(x, y, preferred_element_type=F32)


def kernel(
    spec, leg_hbm, pairs_s, pairs, limits, forcing_hbm, helm, ca, cb, cc, svec, s2vec, vecs,
    grid_out, spec_out,
    leg, forcing, cav, cbv, ccv, spec_t, mix, fac, mul_t, fpad, fsend, rwx, part, prcv, summ, xrcv, xsum,
    xt, tt, smat, s2m, oht, oh, texp, bbuf, brcv, frcv, rwrcv, bd, gbuf, grcv, gout, abuf, ebuf, ercv, fall,
    csem, psem, fs, fr, xs, xr, bs, br, es, er, gs, gr, as_, ar, ws, wr,
):
    lat, lon = lax.axis_index("lat"), lax.axis_index("lon")
    chip, core = lon // 2, lon % 2
    half, field = chip // 4, chip % 4
    partner = 2 * chip + 1 - core
    band, quarter = band_of(lat, half, core)

    barrier = pltpu.get_barrier_semaphore()

    def greet(to_lat, to_lon):
        pl.semaphore_signal(barrier, inc=1, device_id=(to_lat, to_lon), device_id_type=MESH)

    greet(lat, partner)

    @pl.loop(1, 8)
    def _(t):
        greet(lat, 2 * ((chip + t) % 8) + core)

    @pl.loop(0, 16)
    def _(n):
        to_lat, to_lon = owner_of(lat, n // 4, n % 4)

        @pl.when(jnp.logical_or(to_lat != lat, to_lon != lon))
        def _():
            greet(to_lat, to_lon)

        @pl.when(jnp.logical_or(band != lat, n != lon))
        def _():
            greet(band, n)

    @pl.loop(1, 64)
    def _(t):
        greet((lat + t) % 64, lon)

    loads = [
        pltpu.make_async_copy(src, dst, csem.at[n])
        for n, (src, dst) in enumerate(
            [(leg_hbm, leg), (forcing_hbm, forcing), (ca, cav), (cb, cbv), (cc, ccv)]
        )
    ]
    for copy in loads:
        copy.start()

    row, col = iota((64, 84), 0), iota((64, 84), 1) + lon * 84
    second_wave, hemi_row = row % 2 == 1, row // 32 == 1
    pick = (row[:, :8] // 8 % 4 * 2 + row[:, :8] // 2 % 2 == iota((64, 8), 1)).astype(F32)
    low_col = iota((8, 84), 1) + lon * 84
    field_row = iota((8, 84), 0) // 2
    helm_row = jnp.full((8, 84), helm[3])
    for f in range(3):
        helm_row = jnp.where(field_row == f, helm[f], helm_row)

    @pl.loop(0, 10)
    def _(s):
        v = pairs_s[10 * lat + s]
        for f in range(4):
            spec_t[s, 2 * f : 2 * f + 2, :] = spec[f, s]
        edge = M - v
        first = col < edge
        second = jnp.logical_and(col < M + 1, jnp.logical_not(first))
        odd = jnp.where(first, col, col - edge) % 2 == 1
        used = jnp.logical_or(
            jnp.logical_and(second_wave, second), jnp.logical_and(jnp.logical_not(second_wave), first)
        )
        used = jnp.logical_and(used, row // 4 % 2 == s % 2)
        factor = jnp.where(used, jnp.where(jnp.logical_and(hemi_row, odd), -1.0, 1.0), 0.0)
        rounded = spec_t[s].astype(BF16).astype(F32)
        mix[s] = (factor * dot(pick, rounded)).astype(BF16)
        fac[s] = factor * math.sqrt(M)
        degree = jnp.where(low_col < edge, v + low_col, low_col - 1).astype(F32)
        valid = (low_col < M + 1).astype(F32)
        mul_t[s] = valid / (1.0 + helm_row * (degree * (degree + 1.0)))

    loads[0].wait()

    @pl.loop(0, 5)
    def _(sp):
        terms = dot(mix[2 * sp], leg[2 * sp]) + dot(mix[2 * sp + 1], leg[2 * sp + 1])
        terms = (terms * (0.5 / math.sqrt(M))).astype(BF16)
        part[:, :, sp] = terms.reshape(2, 4, 8, M)

    loads[1].wait()
    fpad[...] = jnp.zeros_like(fpad)
    for f in range(4):
        for w in range(4):
            fpad[f, w, 0:10, :] = forcing[f, 10 * w : 10 * w + 10, :]
    fsend[...] = fpad[...].astype(BF16)
    rwx[...] = jnp.zeros_like(rwx)
    rwx[:, 0:40] = jnp.broadcast_to(limits[...].astype(F32), (8, 40))

    my_slot_lat, my_slot_lon = owner_of(lat, 0, field)
    is_self = jnp.logical_and(my_slot_lat == lat, my_slot_lon == lon)
    pl.semaphore_wait(barrier, 103 - 2 * is_self.astype(I32))

    swap = pltpu.make_async_remote_copy(
        part.at[1 - core], prcv, psem.at[0], psem.at[1], device_id=(lat, partner), device_id_type=MESH
    )
    swap.start()

    def forcing_copy(n):
        to_lat, to_lon = owner_of(lat, n // 4, n % 4)
        away = jnp.logical_or(to_lat != lat, to_lon != lon)
        src, dst = fsend.at[n % 4, n // 4], frcv.at[lon]
        remote = pltpu.make_async_remote_copy(
            src, dst, fs.at[n], fr.at[0], device_id=(to_lat, to_lon), device_id_type=MESH
        )
        return away, remote, pltpu.make_async_copy(src, dst, fr.at[0])

    def rows_copy():
        to_lat, to_lon = owner_of(lat, lon // 4, lon % 4)
        away = jnp.logical_or(to_lat != lat, to_lon != lon)
        remote = pltpu.make_async_remote_copy(
            rwx, rwrcv, ws, wr, device_id=(to_lat, to_lon), device_id_type=MESH
        )
        return away, remote, pltpu.make_async_copy(rwx, rwrcv, wr)

    def launch(away, remote, local):
        @pl.when(away)
        def _():
            remote.start()

        @pl.when(jnp.logical_not(away))
        def _():
            local.start()

    @pl.loop(0, 16)
    def _(n):
        launch(*forcing_copy(n))

    launch(*rows_copy())

    swap.wait_recv()
    summ[...] = (part[core].astype(F32) + prcv[...].astype(F32)).astype(BF16)

    step = jnp.where(core == 0, 1, 7)

    def chunk(to):
        return summ.at[to % 4, :, :, pl.ds(pl.multiple_of(640 * (to // 4), 128), 640)]

    def shared(slot, owner, via, src=None):
        src = chunk((chip + owner * step) % 8) if src is None else src
        to = (chip + via * step) % 8
        return pltpu.make_async_remote_copy(
            src, xrcv.at[slot], xs.at[slot], xr.at[slot],
            device_id=(lat, 2 * to + core), device_id_type=MESH,
        )

    opening = [shared(4, 4, 2), shared(3, 3, 1), shared(5, 5, 7), shared(1, 1, 1), shared(7, 7, 7)]
    for copy in opening:
        copy.start()

    lanes = iota((128, 512), 0)
    for i in range(10):
        smat[i] = (svec[core, i : i + 1, :] == lanes).astype(BF16)

    opening[1].wait_recv()
    opening[0].wait_recv()
    onward = chunk((chip + 2 * step) % 8)[...].astype(F32) + xrcv[3].astype(F32) + xrcv[4].astype(F32)
    xsum[0] = onward.astype(BF16)
    ahead = shared(2, 2, 2, xsum.at[0])
    ahead.start()
    opening[2].wait_recv()
    onward = chunk((chip + 6 * step) % 8)[...].astype(F32) + xrcv[5].astype(F32)
    xsum[1] = onward.astype(BF16)
    behind = shared(6, 6, 6, xsum.at[1])
    behind.start()

    expand = (vecs[0:1, :] == iota((128, M), 0)).astype(BF16)
    loads[2].wait()
    base = cav[BASE : BASE + 640, 0:128]
    texp[...] = dot(base, expand).astype(BF16)
    waves = jnp.broadcast_to(pairs[...], (16, 640))
    top = iota((16, 640), 0)
    waves = jnp.where(top == 0, waves // 16, jnp.where(top == 1, waves % 16, 0)).astype(F32).astype(BF16)
    where_from = vecs[1:2, 0:768]
    placed = dot(waves, (where_from == iota((640, 768), 0)).astype(BF16))
    place = jnp.where(where_from >= 0, 40.0 * placed[1:2] + placed[0:1], -1.0)
    for s3 in range(3):
        oht[s3] = (place[:, 256 * s3 : 256 * s3 + 256] == iota((640, 256), 0).astype(F32)).astype(BF16)
    for k in range(6):
        across_rows = jnp.broadcast_to(place[:, 128 * k : 128 * k + 128], (128, 128)).T
        for t in range(5):
            oh[128 * k : 128 * k + 128, 128 * t : 128 * t + 128] = (
                across_rows == (iota((128, 128), 1) + 128 * t).astype(F32)
            ).astype(BF16)
    s2m[...] = (s2vec[core, 0:1, :] == iota((512, M), 0)).astype(BF16)

    total = summ[field, :, :, pl.ds(pl.multiple_of(640 * half, 128), 640)].astype(F32)
    opening[3].wait_recv()
    opening[4].wait_recv()
    ahead.wait_recv()
    behind.wait_recv()
    for slot in (1, 7, 2, 6):
        total = total + xrcv[slot].astype(F32)
    xt[0:40, :] = total.reshape(40, 640)
    xt[40:128, :] = jnp.zeros((88, 640), F32)
    tt[...] = xt[...].T
    packed = dot(tt[pl.ds(0, 64, stride=10), :].astype(BF16), smat[0])
    for i in range(1, 10):
        packed += dot(tt[pl.ds(i, 64, stride=10), :].astype(BF16), smat[i])
    for j in range(4):
        bbuf[:, j, :] = packed[:, 128 * j : 128 * j + 128]

    def to_lines(t):
        to = (lat + t) % 64
        return pltpu.make_async_remote_copy(
            bbuf.at[block_of(to, half, core)], brcv.at[lat], bs, br, device_id=(to, lon), device_id_type=MESH
        )

    @pl.loop(1, 64)
    def _(t):
        to_lines(t).start()

    pltpu.make_async_copy(bbuf.at[block_of(lat, half, core)], brcv.at[lat], br).start()
    pltpu.make_async_copy(frcv, frcv, fr.at[0]).wait()
    push = frcv[...].astype(F32).reshape(256, SEG).T
    pltpu.make_async_copy(rwrcv, rwrcv, wr).wait()
    chosen = (iota((128, 768), 0) == vecs[2:3, 0:768] + 10 * quarter).astype(F32)
    bound = jnp.dot(rwrcv[...], chosen, preferred_element_type=F32, precision=lax.Precision.HIGHEST)
    loads[3].wait()
    loads[4].wait()
    pltpu.make_async_copy(brcv, brcv, br).wait()

    rows = jnp.concatenate([brcv[:, j, :].astype(BF16) for j in range(4)], axis=0)
    coef = jnp.zeros((640, 240), F32)
    for s3 in range(3):
        spread = dot(rows, cav[REP + 128 * s3 : REP + 128 * s3 + 128, :240]).astype(BF16)
        coef += dot(oht[s3], spread)
    lane = iota((40, 240), 1)
    for b in range(16):
        m = iota((40, 240), 0) * 16 + b
        m = jnp.where(lane % 2 == 1, M - 1 - m, m)
        low = 40 * (b % 6)
        keep = jnp.logical_and(lane >= low, lane < low + 40)
        keep = jnp.logical_and(keep, m.astype(F32) < bound[0:1, 0:240])
        value = jnp.where(keep, coef[40 * b : 40 * b + 40], 0.0)
        if b == 0:
            value = jnp.where(m == 0, 0.5 * value, value)
        bd[40 * b : 40 * b + 40, :] = value.astype(BF16)

    sign = jnp.where(iota((1, 240), 1) % 2 == 1, -1.0, 1.0)
    y = jnp.zeros((SEG, 256), F32)
    for g, depth in enumerate((240, 240, 160)):
        cs = dot(cav[T2 : T2 + 640, :depth], bd[240 * g : 240 * g + depth, :])
        c, s = cs[:SEG], cs[SEG:] * sign
        ta = texp[0:SEG, 256 * g : 256 * g + 240].astype(F32)
        tb = texp[SEG:640, 256 * g : 256 * g + 240].astype(F32)
        y += dot((ta * c - tb * s).astype(BF16), cav[W1 + 240 * g : W1 + 240 * g + 240, :])
        y += dot((tb * c + ta * s).astype(BF16), cav[W2 + 240 * g : W2 + 240 * g + 240, :])
    tend = (push - 0.5 * y * y).astype(BF16)
    gbuf[...] = y.T.astype(BF16).reshape(16, 16, SEG)

    gc, gi = dot(tend, cbv[0:256, :]), dot(tend, cbv[256:512, :])
    ta, tb = texp[0:SEG, 768:M].astype(F32), texp[SEG:640, 768:M].astype(F32)
    kc = dot(ccv[...], (ta * gc + tb * gi).astype(BF16))
    ks = dot(ccv[...], (ta * gi - tb * gc).astype(BF16))
    lane = iota((40, 512), 1)
    sign = jnp.where(lane % 2 == 1, -1.0, 1.0)
    m = iota((40, 512), 0) * 16 + lane // 32
    m = jnp.where(lane % 2 == 1, M - 1 - m, m)
    scale = jnp.where(m.astype(F32) < bound[0:1, 256:768], 1.0 / NLON, 0.0)
    real = (kc[:40] + sign * ks[40:]) * scale
    imag = (ks[:40] - sign * kc[40:]) * scale
    lane = iota((40, 128), 1)
    for b in range(16):
        tile, off = 128 * (b // 4), 32 * (b % 4)
        re, im = real[:, tile : tile + 128], imag[:, tile : tile + 128]
        re = pltpu.roll(re, (128 - off) % 128, 1) if off else re
        im = pltpu.roll(im, (148 - off) % 128, 1)
        value = jnp.where(lane < 20, re, jnp.where(lane < 40, im, 0.0))
        abuf[0, 40 * b : 40 * b + 40, :] = value.astype(BF16)
        abuf[1, 40 * b : 40 * b + 40, :] = pltpu.roll(value, 40, 1).astype(BF16)
        abuf[2, 40 * b : 40 * b + 40, :] = pltpu.roll(value, 80, 1).astype(BF16)
    back = jnp.zeros((256, 128), F32)
    for s3 in range(3):
        back += dot(oh[256 * s3 : 256 * s3 + 256, :], abuf[s3])
    for j in range(4):
        ebuf[:, j, :] = back[64 * j : 64 * j + 64]

    block = block_of(lat, half, core)

    def to_waves(t):
        to = (lat + t) % 64
        return pltpu.make_async_remote_copy(
            ebuf.at[to], ercv.at[block], es, er, device_id=(to, lon), device_id_type=MESH
        )

    @pl.loop(1, 64)
    def _(t):
        to_waves(t).start()

    pltpu.make_async_copy(ebuf.at[lat], ercv.at[block], er).start()

    def grid_copy(n):
        away = jnp.logical_or(band != lat, n != lon)
        src, dst = gbuf.at[n], grcv.at[field, quarter]
        remote = pltpu.make_async_remote_copy(
            src, dst, gs.at[n], gr, device_id=(band, n), device_id_type=MESH
        )
        return away, remote, pltpu.make_async_copy(src, dst, gr)

    @pl.loop(0, 16)
    def _(n):
        launch(*grid_copy(n))

    pltpu.make_async_copy(ercv, ercv, er).wait()
    rows = jnp.concatenate([ercv[:, j, :].astype(BF16) for j in range(4)], axis=1)
    placed = dot(rows, s2m[...])
    for i in range(10):
        tt[pl.ds(i, 64, stride=10), :] = placed[:, 128 * i : 128 * i + 128]
    xt[...] = tt[...].T
    fall[core, chip] = xt[0:40, :].astype(BF16).reshape(5, 8, 640)

    def held(k):
        return fall.at[core, (chip + 64 - k * step) % 8]

    def around(k, have):
        to = (chip + (k - have + 8) * step) % 8
        return pltpu.make_async_remote_copy(
            held(have), held(have), as_.at[k], ar.at[k], device_id=(lat, 2 * to + core), device_id_type=MESH
        )

    def across(k):
        return pltpu.make_async_remote_copy(
            held(k), held(k), as_.at[8 + k], ar.at[8 + k], device_id=(lat, partner), device_id_type=MESH
        )

    hops = {2: 0, 6: 0, 1: 0, 7: 0, 4: 2, 3: 2, 5: 6}

    def arrived(k):
        pltpu.make_async_copy(held(k), held(k), ar.at[k]).wait()

    for k in (2, 6, 1, 7):
        around(k, 0).start()
    across(0).start()
    arrived(2)
    around(4, 2).start()
    around(3, 2).start()
    across(2).start()
    arrived(6)
    around(5, 6).start()
    across(6).start()
    for k in (1, 7, 3, 5, 4):
        arrived(k)
        across(k).start()
    for k in range(8):
        pltpu.make_async_copy(held(k), held(k), ar.at[8 + k]).wait()

    nt = (((1,), (1,)), ((), ()))
    of_row = iota((8, 64), 1)
    fold = (of_row // 8 % 4 * 2 + of_row // 2 % 2 == iota((8, 64), 0)).astype(F32)

    @pl.loop(0, 5)
    def _(sp):
        lows, highs = fall[:, 0:4, sp], fall[:, 4:8, sp]
        low = lows.astype(F32).reshape(64, 640).astype(BF16)
        high = highs.astype(F32).reshape(64, 640).astype(BF16)
        for s2 in range(2):
            basis = leg[2 * sp + s2]
            sums = lax.dot_general(low, basis[:, :640], nt, preferred_element_type=F32)
            sums += lax.dot_general(high, basis[:, 640:], nt, preferred_element_type=F32)
            sums = sums * fac[2 * sp + s2]
            folded = jnp.dot(fold, sums, preferred_element_type=F32, precision=lax.Precision.HIGHEST)
            done = (spec_t[2 * sp + s2] + folded) * mul_t[2 * sp + s2]
            for f in range(4):
                spec_out[f, 2 * sp + s2] = done[2 * f : 2 * f + 2]

    pltpu.make_async_copy(grcv, grcv, gr).wait()
    for f in range(4):
        for w in range(4):
            gout[f, 10 * w : 10 * w + 10, :] = grcv[f, w].astype(F32)[:10]
    grid_out[...] = gout[...].astype(BF16)

    swap.wait_send()
    for copy in opening + [ahead, behind]:
        copy.wait_send()
    for k, have in hops.items():
        around(k, have).wait_send()
    for k in range(8):
        across(k).wait_send()
    rest = brcv.at[pl.ds(0, 63)]
    pltpu.make_async_copy(rest, rest, bs).wait()
    pltpu.make_async_copy(rest, rest, es).wait()

    @pl.loop(0, 16)
    def _(n):
        away, remote, _ = forcing_copy(n)

        @pl.when(away)
        def _():
            remote.wait_send()

        away, remote, _ = grid_copy(n)

        @pl.when(away)
        def _():
            remote.wait_send()

    away, remote, _ = rows_copy()

    @pl.when(away)
    def _():
        remote.wait_send()


def body(spec, legendre, wave_pairs, row_waves, forcing, helm_coef):
    vmem, hbm = pl.BlockSpec(memory_space=pltpu.VMEM), pl.BlockSpec(memory_space=pl.ANY)
    smem = pl.BlockSpec(memory_space=pltpu.SMEM)
    dma = pltpu.SemaphoreType.DMA

    def v16(*shape):
        return pltpu.VMEM(shape, BF16)

    def v32(*shape):
        return pltpu.VMEM(shape, F32)

    grid_field, spec_new = pl.pallas_call(
        kernel,
        out_shape=(
            jax.ShapeDtypeStruct((4, 40, SEG), BF16),
            jax.ShapeDtypeStruct((4, 10, 2, 84), F32),
        ),
        in_specs=[vmem, hbm, smem, vmem, vmem, hbm, smem, hbm, hbm, hbm, vmem, vmem, vmem],
        out_specs=(vmem, vmem),
        scratch_shapes=[
            v16(10, 84, M), v32(4, 40, SEG), v16(3104, 256), v16(512, 512), v16(80, SEG), v32(10, 8, 84),
            v16(10, 64, 84), v32(10, 64, 84), v32(10, 8, 84), v32(4, 4, 16, SEG), v16(4, 4, 16, SEG), v32(8, 128),
            v16(2, 4, 5, 8, M), v16(4, 5, 8, M), v16(4, 5, 8, M), v16(8, 5, 8, 640), v16(2, 5, 8, 640),
            v32(128, 640), v32(640, 128), v16(10, 128, 512), v16(512, M), v16(3, 640, 256), v16(768, 640),
            v16(640, M), v32(64, 4, 128), v32(64, 4, 128), v16(16, 16, SEG), v32(8, 128), v16(640, 240),
            v16(16, 16, SEG), v16(4, 4, 16, SEG), v32(4, 40, SEG), v16(3, 640, 128), v32(64, 4, 128),
            v32(64, 4, 128), v16(2, 8, 5, 8, 640),
            dma((5,)), dma((2,)), dma((16,)), dma((1,)), dma((8,)), dma((8,)), dma, dma, dma, dma,
            dma((16,)), dma, dma((16,)), dma((16,)), dma, dma,
        ],
        compiler_params=pltpu.CompilerParams(
            collective_id=0, has_side_effects=True, vmem_limit_bytes=60 * 1024 * 1024
        ),
        name="step",
    )(
        jnp.transpose(spec, (0, 2, 1, 3)), legendre, wave_pairs, wave_pairs.reshape(1, 640),
        row_waves.reshape(1, 40), forcing, helm_coef, *tables(),
    )
    return (grid_field.astype(F32), jnp.transpose(spec_new, (0, 2, 1, 3)))


def solution(mesh):
    return jax.shard_map(
        body,
        mesh=mesh,
        in_specs=(
            P(None, None, "lat", "lon"),
            P("lat", "lon", None),
            P(),
            P("lat"),
            P(None, "lat", "lon"),
            P(),
        ),
        out_specs=(P(None, "lat", "lon"), P(None, None, "lat", "lon")),
        check_vma=False,
    )
```

time: 96.6 us -> 87.3 us (0.904)
  local copies, waits for them, and re-layouts: 9.74 us -> 2.67 us
  other arithmetic: 5.1 us -> 1.61 us
  Pallas kernels: 80.5 us -> 82.1 us
    broadcast_in_dim x8 -> x0, local copies, waits for them, and re-layouts: 3.77 us -> none  [the longest x2 1 us: body(): wcol = jnp.broadcast_to(place.reshape(768, 1), (768, 128))]
    pallas_call x1, Pallas kernels: 80.5 us -> 82.1 us  [body(): pl.pallas_call(kernel, out_shape=(jax.ShapeDtypeStruct((4, 40, SEG), BF16...]
    transpose x2 -> x0, local copies, waits for them, and re-layouts: 1.41 us -> none  [the longest x1 1.41 us: body(): spec_t = jnp.transpose(spec, (2, 0, 1, 3))]
    convert_element_type x6 -> x1, other arithmetic: 2.62 us -> 1.61 us  [body(): return (grid_field.astype(F32), jnp.transpose(spec_new, (0, 2, 1, 3)))]
where the time goes in v2:
time: 87.3 us; the launch traced here: 87 us
  Pallas kernels  82.1 us (94%)
  local copies, waits for them, and re-layouts  2.67 us (3%)
  other arithmetic  1.61 us (2%)
    pallas_call x1, Pallas kernels, body(): pl.pallas_call(kernel, out_shape=(jax.ShapeDtypeStruct((4, 40, SEG), BF16...  82.1 us

profile of v2, /device:TPU:1, one launch (start us, length us, event | category | flops | bytes accessed | tf_op | source)
XLA Modules:
  0.0 87.0 jit_solution(17938290722899935026)
XLA Ops:
  0.6 1.3 %reshape.10.pairs = s32[1,640]{1,0:T(1,128)} reshape(s32[640]{0:T(1024)} %pairs_s.1) | data formatting | bytes 5120 | tf_op jit(solution)/shard_map/reshape | solution.py:561
  1.9 82.1 %step.1 = (bf16[4,40,320]{2,1,0:T(8,128)(2,1)}, f32[4,10,2,84]{3,2,1,0:T(2,128)}) custom-call(f32[4,10,2,84]{3,2,1,0:T(2,128)} %bitcast.3, bf16[10,84,1280]{2,1,0:T(8,128)(2,1)} %leg_hbm.1, s32[640]{0:T(1024)} %pairs_s.1, s32[1,640]{1,0:T(1,128)} %reshape.10.pairs, s32[1,40]{1,0:T(1,128)} %bitcast.5, f32[4,40,320]{2,1,0:T(8,128)} %forcing_hbm.1, f32[4]{0:T(128)} %helm.1, ...), custom_call_target="tpu_custom_call" | custom-call | tf_op jit(solution)/shard_map/step/pallas_call | solution.py:537
  84.0 1.6 %convert_element_type.3 = f32[4,40,320]{2,1,0:T(8,128)} convert(bf16[4,40,320]{2,1,0:T(8,128)(2,1)} %get-tuple-element.4) | non-fusion elementwise | flops 51200 | bytes 307200 | tf_op jit(solution)/shard_map/convert_element_type | solution.py:564
  85.6 1.4 %copy.15 = f32[4,2,10,84]{3,1,2,0:T(2,128)} copy(f32[4,2,10,84]{3,1,2,0:T(2,128)} %bitcast.4) | data formatting | bytes 53760

commit v3 on v2

--- a/solution.py
+++ b/solution.py
@@ -80,28 +80,34 @@
 T2, BASE, W1, W2, REP = 0, 640, 1280, 2000, 2720
 
 
-def band_of(lat, half, hemi):
-    z, y = lat // 8, lat % 8
+def div(a, n):
+    return lax.div(a, jnp.int32(n))
+
+
+def mod(a, n):
+    return lax.rem(a, jnp.int32(n))
+
+
+def band_of(z, y, half, hemi):
     even = jnp.where(hemi == 0, 2 * half, 6 - 2 * half)
-    delta = (z - even + 8) % 8
+    delta = mod(z - even + 8, 8)
     near = jnp.logical_and(delta >= 1, delta <= 4)
     band = jnp.where(near, even + 1, even) * 8 + y
-    quarter = jnp.where(near, delta - 1, (8 - delta) % 8)
+    quarter = jnp.where(near, delta - 1, mod(8 - delta, 8))
     return band, quarter
 
 
-def block_of(lat, half, hemi):
-    band, quarter = band_of(lat, half, hemi)
+def block_of(z, y, half, hemi):
+    band, quarter = band_of(z, y, half, hemi)
+    return jnp.where(hemi == 0, 4 * (band - 16 * half) + quarter, 4 * (63 - band - 16 * half) + 3 - quarter)
+
+
+def owner_of(band, quarter, field):
+    hemi = div(band, 32)
     north = jnp.where(hemi == 0, band, 63 - band)
-    return 4 * (north - 16 * half) + jnp.where(hemi == 0, quarter, 3 - quarter)
-
-
-def owner_of(band, quarter, field):
-    hemi = band // 32
-    north = jnp.where(hemi == 0, band, 63 - band)
-    z, y = band // 8, band % 8
-    z = (z + jnp.where(z % 2 == 1, quarter, 8 - quarter)) % 8
-    return z * 8 + y, 2 * (4 * (north // 16) + field) + hemi
+    z, y = div(band, 8), mod(band, 8)
+    z = mod(z + jnp.where(mod(z, 2) == 1, quarter, 8 - quarter), 8)
+    return z * 8 + y, 2 * (4 * div(north, 16) + field) + hemi
 
 
 def iota(shape, dim):
@@ -115,30 +121,39 @@
 def kernel(
     spec, leg_hbm, pairs_s, pairs, limits, forcing_hbm, helm, ca, cb, cc, svec, s2vec, vecs,
     grid_out, spec_out,
-    leg, forcing, cav, cbv, ccv, spec_t, mix, fac, mul_t, fpad, fsend, rwx, part, prcv, summ, xrcv, xsum,
-    xt, tt, smat, s2m, oht, oh, texp, bbuf, brcv, frcv, rwrcv, bd, gbuf, grcv, gout, abuf, ebuf, ercv, fall,
+    leg, forcing, cav, cbv, ccv, spec_t, mix, fac, mul_t, fpad, fsend, fsend2, rwx, part, prcv, summ, xrcv, xsum,
+    xt, tt, smat, s2m, oht, oh, texp, bbuf, brcv, frcv, frcv2, lines, rwrcv, bd, gbuf, gbuf2, grcv, grcv2, abuf, ebuf, ercv, fall,
     csem, psem, fs, fr, xs, xr, bs, br, es, er, gs, gr, as_, ar, ws, wr,
 ):
     lat, lon = lax.axis_index("lat"), lax.axis_index("lon")
-    chip, core = lon // 2, lon % 2
-    half, field = chip // 4, chip % 4
+    chip, core = div(lon, 2), mod(lon, 2)
+    half, field = div(chip, 4), mod(chip, 4)
+    zc, yc = div(lat, 8), mod(lat, 8)
     partner = 2 * chip + 1 - core
-    band, quarter = band_of(lat, half, core)
+    band, quarter = band_of(zc, yc, half, core)
 
     barrier = pltpu.get_barrier_semaphore()
 
     def greet(to_lat, to_lon):
         pl.semaphore_signal(barrier, inc=1, device_id=(to_lat, to_lon), device_id_type=MESH)
 
-    greet(lat, partner)
-
-    @pl.loop(1, 8)
-    def _(t):
-        greet(lat, 2 * ((chip + t) % 8) + core)
+    def far_first(n):
+        return mod(zc + 4 + div(n, 8), 8), mod(yc + 4 + mod(n, 8), 8)
+
+    def others(action):
+        @pl.loop(0, 36)
+        def _(n):
+            action(*far_first(n))
+
+        @pl.loop(37, 64)
+        def _(n):
+            action(*far_first(n))
+
+    others(lambda to_z, to_y: greet(to_z * 8 + to_y, lon))
 
     @pl.loop(0, 16)
     def _(n):
-        to_lat, to_lon = owner_of(lat, n // 4, n % 4)
+        to_lat, to_lon = owner_of(lat, div(n, 4), mod(n, 4))
 
         @pl.when(jnp.logical_or(to_lat != lat, to_lon != lon))
         def _():
@@ -148,9 +163,11 @@
         def _():
             greet(band, n)
 
-    @pl.loop(1, 64)
+    greet(lat, partner)
+
+    @pl.loop(1, 8)
     def _(t):
-        greet((lat + t) % 64, lon)
+        greet(lat, 2 * mod(chip + t, 8) + core)
 
     loads = [
         pltpu.make_async_copy(src, dst, csem.at[n])
@@ -200,11 +217,11 @@
         part[:, :, sp] = terms.reshape(2, 4, 8, M)
 
     loads[1].wait()
-    fpad[...] = jnp.zeros_like(fpad)
     for f in range(4):
         for w in range(4):
             fpad[f, w, 0:10, :] = forcing[f, 10 * w : 10 * w + 10, :]
-    fsend[...] = fpad[...].astype(BF16)
+    fsend[...] = fpad[:, :, 0:8, :].astype(BF16)
+    fsend2[...] = fpad[:, :, 8:10, :].astype(BF16)
     rwx[...] = jnp.zeros_like(rwx)
     rwx[:, 0:40] = jnp.broadcast_to(limits[...].astype(F32), (8, 40))
 
@@ -218,30 +235,41 @@
     swap.start()
 
     def forcing_copy(n):
-        to_lat, to_lon = owner_of(lat, n // 4, n % 4)
+        to_lat, to_lon = owner_of(lat, div(n, 4), mod(n, 4))
         away = jnp.logical_or(to_lat != lat, to_lon != lon)
-        src, dst = fsend.at[n % 4, n // 4], frcv.at[lon]
-        remote = pltpu.make_async_remote_copy(
-            src, dst, fs.at[n], fr.at[0], device_id=(to_lat, to_lon), device_id_type=MESH
-        )
-        return away, remote, pltpu.make_async_copy(src, dst, fr.at[0])
+        pieces = []
+        for n2, (src, dst) in enumerate([(fsend, frcv), (fsend2, frcv2)]):
+            src, dst = src.at[mod(n, 4), div(n, 4)], dst.at[lon]
+            remote = pltpu.make_async_remote_copy(
+                src, dst, fs.at[n2, n], fr.at[n2], device_id=(to_lat, to_lon), device_id_type=MESH
+            )
+            pieces.append((remote, pltpu.make_async_copy(src, dst, fr.at[n2])))
+        return away, pieces
 
     def rows_copy():
-        to_lat, to_lon = owner_of(lat, lon // 4, lon % 4)
+        to_lat, to_lon = owner_of(lat, div(lon, 4), mod(lon, 4))
         away = jnp.logical_or(to_lat != lat, to_lon != lon)
         remote = pltpu.make_async_remote_copy(
             rwx, rwrcv, ws, wr, device_id=(to_lat, to_lon), device_id_type=MESH
         )
-        return away, remote, pltpu.make_async_copy(rwx, rwrcv, wr)
-
-    def launch(away, remote, local):
+        return away, [(remote, pltpu.make_async_copy(rwx, rwrcv, wr))]
+
+    def launch(away, pieces):
         @pl.when(away)
         def _():
-            remote.start()
+            for remote, _ in pieces:
+                remote.start()
 
         @pl.when(jnp.logical_not(away))
         def _():
-            local.start()
+            for _, local in pieces:
+                local.start()
+
+    def settle(away, pieces):
+        @pl.when(away)
+        def _():
+            for remote, _ in pieces:
+                remote.wait_send()
 
     @pl.loop(0, 16)
     def _(n):
@@ -255,11 +283,11 @@
     step = jnp.where(core == 0, 1, 7)
 
     def chunk(to):
-        return summ.at[to % 4, :, :, pl.ds(pl.multiple_of(640 * (to // 4), 128), 640)]
+        return summ.at[mod(to, 4), :, :, pl.ds(pl.multiple_of(640 * div(to, 4), 128), 640)]
 
     def shared(slot, owner, via, src=None):
-        src = chunk((chip + owner * step) % 8) if src is None else src
-        to = (chip + via * step) % 8
+        src = chunk(mod(chip + owner * step, 8)) if src is None else src
+        to = mod(chip + via * step, 8)
         return pltpu.make_async_remote_copy(
             src, xrcv.at[slot], xs.at[slot], xr.at[slot],
             device_id=(lat, 2 * to + core), device_id_type=MESH,
@@ -275,12 +303,12 @@
 
     opening[1].wait_recv()
     opening[0].wait_recv()
-    onward = chunk((chip + 2 * step) % 8)[...].astype(F32) + xrcv[3].astype(F32) + xrcv[4].astype(F32)
+    onward = chunk(mod(chip + 2 * step, 8))[...].astype(F32) + xrcv[3].astype(F32) + xrcv[4].astype(F32)
     xsum[0] = onward.astype(BF16)
     ahead = shared(2, 2, 2, xsum.at[0])
     ahead.start()
     opening[2].wait_recv()
-    onward = chunk((chip + 6 * step) % 8)[...].astype(F32) + xrcv[5].astype(F32)
+    onward = chunk(mod(chip + 6 * step, 8))[...].astype(F32) + xrcv[5].astype(F32)
     xsum[1] = onward.astype(BF16)
     behind = shared(6, 6, 6, xsum.at[1])
     behind.start()
@@ -289,7 +317,8 @@
     loads[2].wait()
     base = cav[BASE : BASE + 640, 0:128]
     texp[...] = dot(base, expand).astype(BF16)
-    waves = jnp.broadcast_to(pairs[...], (16, 640))
+    waves = jnp.concatenate([pairs[t : t + 1, :] for t in range(5)], axis=1)
+    waves = jnp.broadcast_to(waves, (16, 640))
     top = iota((16, 640), 0)
     waves = jnp.where(top == 0, waves // 16, jnp.where(top == 1, waves % 16, 0)).astype(F32).astype(BF16)
     where_from = vecs[1:2, 0:768]
@@ -321,19 +350,20 @@
     for j in range(4):
         bbuf[:, j, :] = packed[:, 128 * j : 128 * j + 128]
 
-    def to_lines(t):
-        to = (lat + t) % 64
-        return pltpu.make_async_remote_copy(
-            bbuf.at[block_of(to, half, core)], brcv.at[lat], bs, br, device_id=(to, lon), device_id_type=MESH
-        )
-
-    @pl.loop(1, 64)
-    def _(t):
-        to_lines(t).start()
-
-    pltpu.make_async_copy(bbuf.at[block_of(lat, half, core)], brcv.at[lat], br).start()
+    def to_lines(to_z, to_y):
+        pltpu.make_async_remote_copy(
+            bbuf.at[block_of(to_z, to_y, half, core)], brcv.at[lat], bs, br,
+            device_id=(to_z * 8 + to_y, lon), device_id_type=MESH,
+        ).start()
+
+    others(to_lines)
+    pltpu.make_async_copy(bbuf.at[block_of(zc, yc, half, core)], brcv.at[lat], br).start()
     pltpu.make_async_copy(frcv, frcv, fr.at[0]).wait()
-    push = frcv[...].astype(F32).reshape(256, SEG).T
+    pltpu.make_async_copy(frcv2, frcv2, fr.at[1]).wait()
+    lines[:, 0:8, :] = frcv[...].astype(F32)
+    lines[:, 8:10, :] = frcv2[...].astype(F32)
+    lines[:, 10:16, :] = jnp.zeros((16, 6, SEG), F32)
+    push = lines[...].reshape(256, SEG).T
     pltpu.make_async_copy(rwrcv, rwrcv, wr).wait()
     chosen = (iota((128, 768), 0) == vecs[2:3, 0:768] + 10 * quarter).astype(F32)
     bound = jnp.dot(rwrcv[...], chosen, preferred_element_type=F32, precision=lax.Precision.HIGHEST)
@@ -368,7 +398,9 @@
         y += dot((ta * c - tb * s).astype(BF16), cav[W1 + 240 * g : W1 + 240 * g + 240, :])
         y += dot((tb * c + ta * s).astype(BF16), cav[W2 + 240 * g : W2 + 240 * g + 240, :])
     tend = (push - 0.5 * y * y).astype(BF16)
-    gbuf[...] = y.T.astype(BF16).reshape(16, 16, SEG)
+    lines[...] = y.T.reshape(16, 16, SEG)
+    gbuf[...] = lines[:, 0:8, :].astype(BF16)
+    gbuf2[...] = lines[:, 8:10, :].astype(BF16)
 
     gc, gi = dot(tend, cbv[0:256, :]), dot(tend, cbv[256:512, :])
     ta, tb = texp[0:SEG, 768:M].astype(F32), texp[SEG:640, 768:M].astype(F32)
@@ -397,27 +429,27 @@
     for j in range(4):
         ebuf[:, j, :] = back[64 * j : 64 * j + 64]
 
-    block = block_of(lat, half, core)
-
-    def to_waves(t):
-        to = (lat + t) % 64
-        return pltpu.make_async_remote_copy(
+    block = block_of(zc, yc, half, core)
+
+    def to_waves(to_z, to_y):
+        to = to_z * 8 + to_y
+        pltpu.make_async_remote_copy(
             ebuf.at[to], ercv.at[block], es, er, device_id=(to, lon), device_id_type=MESH
-        )
-
-    @pl.loop(1, 64)
-    def _(t):
-        to_waves(t).start()
-
+        ).start()
+
+    others(to_waves)
     pltpu.make_async_copy(ebuf.at[lat], ercv.at[block], er).start()
 
     def grid_copy(n):
         away = jnp.logical_or(band != lat, n != lon)
-        src, dst = gbuf.at[n], grcv.at[field, quarter]
-        remote = pltpu.make_async_remote_copy(
-            src, dst, gs.at[n], gr, device_id=(band, n), device_id_type=MESH
-        )
-        return away, remote, pltpu.make_async_copy(src, dst, gr)
+        pieces = []
+        for n2, (src, dst) in enumerate([(gbuf, grcv), (gbuf2, grcv2)]):
+            src, dst = src.at[n], dst.at[field, quarter]
+            remote = pltpu.make_async_remote_copy(
+                src, dst, gs.at[n2, n], gr.at[n2], device_id=(band, n), device_id_type=MESH
+            )
+            pieces.append((remote, pltpu.make_async_copy(src, dst, gr.at[n2])))
+        return away, pieces
 
     @pl.loop(0, 16)
     def _(n):
@@ -432,10 +464,10 @@
     fall[core, chip] = xt[0:40, :].astype(BF16).reshape(5, 8, 640)
 
     def held(k):
-        return fall.at[core, (chip + 64 - k * step) % 8]
+        return fall.at[core, mod(chip + 64 - k * step, 8)]
 
     def around(k, have):
-        to = (chip + (k - have + 8) * step) % 8
+        to = mod(chip + (k - have + 8) * step, 8)
         return pltpu.make_async_remote_copy(
             held(have), held(have), as_.at[k], ar.at[k], device_id=(lat, 2 * to + core), device_id_type=MESH
         )
@@ -485,11 +517,12 @@
             for f in range(4):
                 spec_out[f, 2 * sp + s2] = done[2 * f : 2 * f + 2]
 
-    pltpu.make_async_copy(grcv, grcv, gr).wait()
+    pltpu.make_async_copy(grcv, grcv, gr.at[0]).wait()
+    pltpu.make_async_copy(grcv2, grcv2, gr.at[1]).wait()
     for f in range(4):
         for w in range(4):
-            gout[f, 10 * w : 10 * w + 10, :] = grcv[f, w].astype(F32)[:10]
-    grid_out[...] = gout[...].astype(BF16)
+            grid_out[f, 10 * w : 10 * w + 8, :] = grcv[f, w].astype(F32)
+            grid_out[f, 10 * w + 8 : 10 * w + 10, :] = grcv2[f, w].astype(F32)
 
     swap.wait_send()
     for copy in opening + [ahead, behind]:
@@ -504,23 +537,10 @@
 
     @pl.loop(0, 16)
     def _(n):
-        away, remote, _ = forcing_copy(n)
-
-        @pl.when(away)
-        def _():
-            remote.wait_send()
-
-        away, remote, _ = grid_copy(n)
-
-        @pl.when(away)
-        def _():
-            remote.wait_send()
-
-    away, remote, _ = rows_copy()
-
-    @pl.when(away)
-    def _():
-        remote.wait_send()
+        settle(*forcing_copy(n))
+        settle(*grid_copy(n))
+
+    settle(*rows_copy())
 
 
 def body(spec, legendre, wave_pairs, row_waves, forcing, helm_coef):
@@ -537,31 +557,31 @@
     grid_field, spec_new = pl.pallas_call(
         kernel,
         out_shape=(
-            jax.ShapeDtypeStruct((4, 40, SEG), BF16),
-            jax.ShapeDtypeStruct((4, 10, 2, 84), F32),
+            v32(4, 40, SEG),
+            v32(4, 10, 2, 84),
         ),
         in_specs=[vmem, hbm, smem, vmem, vmem, hbm, smem, hbm, hbm, hbm, vmem, vmem, vmem],
         out_specs=(vmem, vmem),
         scratch_shapes=[
             v16(10, 84, M), v32(4, 40, SEG), v16(3104, 256), v16(512, 512), v16(80, SEG), v32(10, 8, 84),
-            v16(10, 64, 84), v32(10, 64, 84), v32(10, 8, 84), v32(4, 4, 16, SEG), v16(4, 4, 16, SEG), v32(8, 128),
+            v16(10, 64, 84), v32(10, 64, 84), v32(10, 8, 84), v32(4, 4, 16, SEG), v16(4, 4, 8, SEG), v16(4, 4, 2, SEG), v32(8, 128),
             v16(2, 4, 5, 8, M), v16(4, 5, 8, M), v16(4, 5, 8, M), v16(8, 5, 8, 640), v16(2, 5, 8, 640),
             v32(128, 640), v32(640, 128), v16(10, 128, 512), v16(512, M), v16(3, 640, 256), v16(768, 640),
-            v16(640, M), v32(64, 4, 128), v32(64, 4, 128), v16(16, 16, SEG), v32(8, 128), v16(640, 240),
-            v16(16, 16, SEG), v16(4, 4, 16, SEG), v32(4, 40, SEG), v16(3, 640, 128), v32(64, 4, 128),
+            v16(640, M), v32(64, 4, 128), v32(64, 4, 128), v16(16, 8, SEG), v16(16, 2, SEG), v32(16, 16, SEG), v32(8, 128),
+            v16(640, 240), v16(16, 8, SEG), v16(16, 2, SEG), v16(4, 4, 8, SEG), v16(4, 4, 2, SEG), v16(3, 640, 128), v32(64, 4, 128),
             v32(64, 4, 128), v16(2, 8, 5, 8, 640),
-            dma((5,)), dma((2,)), dma((16,)), dma((1,)), dma((8,)), dma((8,)), dma, dma, dma, dma,
-            dma((16,)), dma, dma((16,)), dma((16,)), dma, dma,
+            dma((5,)), dma((2,)), dma((2, 16)), dma((2,)), dma((8,)), dma((8,)), dma, dma, dma, dma,
+            dma((2, 16)), dma((2,)), dma((16,)), dma((16,)), dma, dma,
         ],
         compiler_params=pltpu.CompilerParams(
             collective_id=0, has_side_effects=True, vmem_limit_bytes=60 * 1024 * 1024
         ),
         name="step",
     )(
-        jnp.transpose(spec, (0, 2, 1, 3)), legendre, wave_pairs, wave_pairs.reshape(1, 640),
+        jnp.transpose(spec, (0, 2, 1, 3)), legendre, wave_pairs, wave_pairs.reshape(5, 128),
         row_waves.reshape(1, 40), forcing, helm_coef, *tables(),
     )
-    return (grid_field.astype(F32), jnp.transpose(spec_new, (0, 2, 1, 3)))
+    return (grid_field, jnp.transpose(spec_new, (0, 2, 1, 3)))
 
 
 def solution(mesh):

time: 87.3 us -> 80.2 us (0.919)
  Pallas kernels: 82.1 us -> 78.1 us
  other arithmetic: 1.61 us -> 0 us
  local copies, waits for them, and re-layouts: 2.67 us -> 1.31 us
    pallas_call x1, Pallas kernels: 82.1 us -> 78.1 us  [body(): pl.pallas_call(kernel, out_shape=(v32(4, 40, SEG), v32(4, 10, 2, 84)), in...]
    convert_element_type x1 -> x0, other arithmetic: 1.61 us -> none  [body(): return (grid_field.astype(F32), jnp.transpose(spec_new, (0, 2, 1, 3)))]
    reshape x1 -> x0, local copies, waits for them, and re-layouts: 1.27 us -> none  [body(): wave_pairs.reshape(1, 640)]
where the time goes in v3:
time: 80.2 us; the launch traced here: 80 us
  Pallas kernels  78.1 us (97%)
  local copies, waits for them, and re-layouts  1.31 us (2%)
    pallas_call x1, Pallas kernels, body(): pl.pallas_call(kernel, out_shape=(v32(4, 40, SEG), v32(4, 10, 2, 84)), in...  78.1 us

profile of v3, /device:TPU:1, one launch (start us, length us, event | category | flops | bytes accessed | tf_op | source)
XLA Modules:
  0.0 80.0 jit_solution(5173894439415991063)
XLA Ops:
  0.6 78.1 %step.1 = (f32[4,40,320]{2,1,0:T(8,128)S(1)}, f32[4,10,2,84]{3,2,1,0:T(2,128)S(1)}) custom-call(f32[4,10,2,84]{3,2,1,0:T(2,128)} %bitcast.5, bf16[10,84,1280]{2,1,0:T(8,128)(2,1)} %leg_hbm.1, s32[640]{0:T(1024)} %pairs_s.1, s32[5,128]{1,0:T(8,128)} %bitcast.6, s32[1,40]{1,0:T(1,128)} %bitcast.7, f32[4,40,320]{2,1,0:T(8,128)} %forcing_hbm.1, f32[4]{0:T(128)} %helm.1, ...), custom_call_target="tpu_custom_call" | custom-call | tf_op jit(solution)/shard_map/step/pallas_call | solution.py:557
  78.7 0.7 copy.16
  79.4 0.6 copy.17

commit v4 on v3

--- a/solution.py
+++ b/solution.py
@@ -119,9 +119,9 @@
 
 
 def kernel(
-    spec, leg_hbm, pairs_s, pairs, limits, forcing_hbm, helm, ca, cb, cc, svec, s2vec, vecs,
+    leg_hbm, forcing_hbm, ca, cb, cc, spec_hbm, pairs_hbm, limits_hbm, helm_hbm, svec_hbm, s2vec_hbm, vecs_hbm,
     grid_out, spec_out,
-    leg, forcing, cav, cbv, ccv, spec_t, mix, fac, mul_t, fpad, fsend, fsend2, rwx, part, prcv, summ, xrcv, xsum,
+    leg, forcing, cav, cbv, ccv, spec, pairs, limits, helm, svec, s2vec, vecs, vcol, spec_t, mix, fac, mul_t, fpad, fsend, fsend2, rwx, part, prcv, summ, xrcv, xsum,
     xt, tt, smat, s2m, oht, oh, texp, bbuf, brcv, frcv, frcv2, lines, rwrcv, bd, gbuf, gbuf2, grcv, grcv2, abuf, ebuf, ercv, fall,
     csem, psem, fs, fr, xs, xr, bs, br, es, er, gs, gr, as_, ar, ws, wr,
 ):
@@ -172,24 +172,35 @@
     loads = [
         pltpu.make_async_copy(src, dst, csem.at[n])
         for n, (src, dst) in enumerate(
-            [(leg_hbm, leg), (forcing_hbm, forcing), (ca, cav), (cb, cbv), (cc, ccv)]
+            [
+                (leg_hbm, leg), (forcing_hbm, forcing), (ca, cav), (cb, cbv), (cc, ccv), (spec_hbm, spec),
+                (pairs_hbm, pairs), (limits_hbm, limits), (helm_hbm, helm), (svec_hbm, svec),
+                (s2vec_hbm, s2vec), (vecs_hbm, vecs),
+            ]
         )
     ]
-    for copy in loads:
-        copy.start()
+    for n in (6, 5, 8, 0, 1, 7, 9, 11, 10, 2, 3, 4):
+        loads[n].start()
 
     row, col = iota((64, 84), 0), iota((64, 84), 1) + lon * 84
     second_wave, hemi_row = row % 2 == 1, row // 32 == 1
     pick = (row[:, :8] // 8 % 4 * 2 + row[:, :8] // 2 % 2 == iota((64, 8), 1)).astype(F32)
     low_col = iota((8, 84), 1) + lon * 84
     field_row = iota((8, 84), 0) // 2
-    helm_row = jnp.full((8, 84), helm[3])
+    loads[8].wait()
+    helm_row = jnp.broadcast_to(helm[0:1, 3:4], (8, 84))
     for f in range(3):
-        helm_row = jnp.where(field_row == f, helm[f], helm_row)
+        helm_row = jnp.where(field_row == f, jnp.broadcast_to(helm[0:1, f : f + 1], (8, 84)), helm_row)
+    loads[6].wait()
+    waves = jnp.concatenate([pairs[t : t + 1, :] for t in range(5)], axis=1)
+    ours = iota((16, 640), 1) == iota((16, 640), 0) + 10 * lat
+    ours = jnp.sum(jnp.where(ours, jnp.broadcast_to(waves, (16, 640)).astype(F32), 0.0), axis=1, keepdims=True)
+    vcol[...] = jnp.broadcast_to(ours, (16, 128))
+    loads[5].wait()
 
     @pl.loop(0, 10)
     def _(s):
-        v = pairs_s[10 * lat + s]
+        v = vcol[pl.ds(s, 1), 0:84].astype(I32)
         for f in range(4):
             spec_t[s, 2 * f : 2 * f + 2, :] = spec[f, s]
         edge = M - v
@@ -222,6 +233,7 @@
             fpad[f, w, 0:10, :] = forcing[f, 10 * w : 10 * w + 10, :]
     fsend[...] = fpad[:, :, 0:8, :].astype(BF16)
     fsend2[...] = fpad[:, :, 8:10, :].astype(BF16)
+    loads[7].wait()
     rwx[...] = jnp.zeros_like(rwx)
     rwx[:, 0:40] = jnp.broadcast_to(limits[...].astype(F32), (8, 40))
 
@@ -229,10 +241,17 @@
     is_self = jnp.logical_and(my_slot_lat == lat, my_slot_lon == lon)
     pl.semaphore_wait(barrier, 103 - 2 * is_self.astype(I32))
 
-    swap = pltpu.make_async_remote_copy(
-        part.at[1 - core], prcv, psem.at[0], psem.at[1], device_id=(lat, partner), device_id_type=MESH
-    )
-    swap.start()
+    step = jnp.where(core == 0, 1, 7)
+
+    def swap(n, toward):
+        f = mod(chip + (0, 3, 1, 2)[n] * toward, 4)
+        return pltpu.make_async_remote_copy(
+            part.at[1 - core, f], prcv.at[f], psem.at[0, n], psem.at[1, n],
+            device_id=(lat, partner), device_id_type=MESH,
+        )
+
+    for n in range(4):
+        swap(n, 8 - step).start()
 
     def forcing_copy(n):
         to_lat, to_lon = owner_of(lat, div(n, 4), mod(n, 4))
@@ -277,11 +296,6 @@
 
     launch(*rows_copy())
 
-    swap.wait_recv()
-    summ[...] = (part[core].astype(F32) + prcv[...].astype(F32)).astype(BF16)
-
-    step = jnp.where(core == 0, 1, 7)
-
     def chunk(to):
         return summ.at[mod(to, 4), :, :, pl.ds(pl.multiple_of(640 * div(to, 4), 128), 640)]
 
@@ -294,9 +308,15 @@
         )
 
     opening = [shared(4, 4, 2), shared(3, 3, 1), shared(5, 5, 7), shared(1, 1, 1), shared(7, 7, 7)]
-    for copy in opening:
-        copy.start()
-
+    for n, ready in enumerate(((0,), (1, 4), (2, 3), ())):
+        swap(n, step).wait_recv()
+        f = mod(chip + (0, 3, 1, 2)[n] * step, 4)
+        summ[f] = (part[core, f].astype(F32) + prcv[f].astype(F32)).astype(BF16)
+        for k in ready:
+            opening[k].start()
+
+    for n in (9, 10, 11):
+        loads[n].wait()
     lanes = iota((128, 512), 0)
     for i in range(10):
         smat[i] = (svec[core, i : i + 1, :] == lanes).astype(BF16)
@@ -317,7 +337,6 @@
     loads[2].wait()
     base = cav[BASE : BASE + 640, 0:128]
     texp[...] = dot(base, expand).astype(BF16)
-    waves = jnp.concatenate([pairs[t : t + 1, :] for t in range(5)], axis=1)
     waves = jnp.broadcast_to(waves, (16, 640))
     top = iota((16, 640), 0)
     waves = jnp.where(top == 0, waves // 16, jnp.where(top == 1, waves % 16, 0)).astype(F32).astype(BF16)
@@ -495,6 +514,13 @@
     for k in (1, 7, 3, 5, 4):
         arrived(k)
         across(k).start()
+    pltpu.make_async_copy(grcv, grcv, gr.at[0]).wait()
+    pltpu.make_async_copy(grcv2, grcv2, gr.at[1]).wait()
+    for f in range(4):
+        for w in range(4):
+            grid_out[f, 10 * w : 10 * w + 8, :] = grcv[f, w].astype(F32)
+            grid_out[f, 10 * w + 8 : 10 * w + 10, :] = grcv2[f, w].astype(F32)
+
     for k in range(8):
         pltpu.make_async_copy(held(k), held(k), ar.at[8 + k]).wait()
 
@@ -517,14 +543,8 @@
             for f in range(4):
                 spec_out[f, 2 * sp + s2] = done[2 * f : 2 * f + 2]
 
-    pltpu.make_async_copy(grcv, grcv, gr.at[0]).wait()
-    pltpu.make_async_copy(grcv2, grcv2, gr.at[1]).wait()
-    for f in range(4):
-        for w in range(4):
-            grid_out[f, 10 * w : 10 * w + 8, :] = grcv[f, w].astype(F32)
-            grid_out[f, 10 * w + 8 : 10 * w + 10, :] = grcv2[f, w].astype(F32)
-
-    swap.wait_send()
+    for n in range(4):
+        swap(n, 8 - step).wait_send()
     for copy in opening + [ahead, behind]:
         copy.wait_send()
     for k, have in hops.items():
@@ -545,7 +565,6 @@
 
 def body(spec, legendre, wave_pairs, row_waves, forcing, helm_coef):
     vmem, hbm = pl.BlockSpec(memory_space=pltpu.VMEM), pl.BlockSpec(memory_space=pl.ANY)
-    smem = pl.BlockSpec(memory_space=pltpu.SMEM)
     dma = pltpu.SemaphoreType.DMA
 
     def v16(*shape):
@@ -553,6 +572,9 @@
 
     def v32(*shape):
         return pltpu.VMEM(shape, F32)
+
+    def v_i(*shape):
+        return pltpu.VMEM(shape, I32)
 
     grid_field, spec_new = pl.pallas_call(
         kernel,
@@ -560,17 +582,19 @@
             v32(4, 40, SEG),
             v32(4, 10, 2, 84),
         ),
-        in_specs=[vmem, hbm, smem, vmem, vmem, hbm, smem, hbm, hbm, hbm, vmem, vmem, vmem],
+        in_specs=[hbm] * 12,
         out_specs=(vmem, vmem),
         scratch_shapes=[
-            v16(10, 84, M), v32(4, 40, SEG), v16(3104, 256), v16(512, 512), v16(80, SEG), v32(10, 8, 84),
+            v16(10, 84, M), v32(4, 40, SEG), v16(3104, 256), v16(512, 512), v16(80, SEG),
+            v32(4, 10, 2, 84), v_i(5, 128), v_i(1, 40), v32(1, 4), v_i(2, 16, 512), v_i(2, 8, M), v_i(8, M),
+            v32(16, 128), v32(10, 8, 84),
             v16(10, 64, 84), v32(10, 64, 84), v32(10, 8, 84), v32(4, 4, 16, SEG), v16(4, 4, 8, SEG), v16(4, 4, 2, SEG), v32(8, 128),
             v16(2, 4, 5, 8, M), v16(4, 5, 8, M), v16(4, 5, 8, M), v16(8, 5, 8, 640), v16(2, 5, 8, 640),
             v32(128, 640), v32(640, 128), v16(10, 128, 512), v16(512, M), v16(3, 640, 256), v16(768, 640),
             v16(640, M), v32(64, 4, 128), v32(64, 4, 128), v16(16, 8, SEG), v16(16, 2, SEG), v32(16, 16, SEG), v32(8, 128),
             v16(640, 240), v16(16, 8, SEG), v16(16, 2, SEG), v16(4, 4, 8, SEG), v16(4, 4, 2, SEG), v16(3, 640, 128), v32(64, 4, 128),
             v32(64, 4, 128), v16(2, 8, 5, 8, 640),
-            dma((5,)), dma((2,)), dma((2, 16)), dma((2,)), dma((8,)), dma((8,)), dma, dma, dma, dma,
+            dma((12,)), dma((2, 4)), dma((2, 16)), dma((2,)), dma((8,)), dma((8,)), dma, dma, dma, dma,
             dma((2, 16)), dma((2,)), dma((16,)), dma((16,)), dma, dma,
         ],
         compiler_params=pltpu.CompilerParams(
@@ -578,8 +602,8 @@
         ),
         name="step",
     )(
-        jnp.transpose(spec, (0, 2, 1, 3)), legendre, wave_pairs, wave_pairs.reshape(5, 128),
-        row_waves.reshape(1, 40), forcing, helm_coef, *tables(),
+        legendre, forcing, *tables()[:3], jnp.transpose(spec, (0, 2, 1, 3)), wave_pairs.reshape(5, 128),
+        row_waves.reshape(1, 40), helm_coef.reshape(1, 4), *tables()[3:],
     )
     return (grid_field, jnp.transpose(spec_new, (0, 2, 1, 3)))
 

time: 80.2 us -> 78.8 us (0.983)
  Pallas kernels: 78.1 us -> 76.7 us
    pallas_call x1, Pallas kernels: 78.1 us -> 76.7 us  [body(): pl.pallas_call(kernel, out_shape=(v32(4, 40, SEG), v32(4, 10, 2, 84)), in...]
where the time goes in v4:
time: 78.8 us; the launch traced here: 78.7 us
  Pallas kernels  76.7 us (97%)
  local copies, waits for them, and re-layouts  1.31 us (2%)
    pallas_call x1, Pallas kernels, body(): pl.pallas_call(kernel, out_shape=(v32(4, 40, SEG), v32(4, 10, 2, 84)), in...  76.7 us

profile of v4, /device:TPU:1, one launch (start us, length us, event | category | flops | bytes accessed | tf_op | source)
XLA Modules:
  0.0 78.7 jit_solution(11460553681737041614)
XLA Ops:
  0.6 76.7 %step.1 = (f32[4,40,320]{2,1,0:T(8,128)S(1)}, f32[4,10,2,84]{3,2,1,0:T(2,128)S(1)}) custom-call(bf16[10,84,1280]{2,1,0:T(8,128)(2,1)} %leg_hbm.1, f32[4,40,320]{2,1,0:T(8,128)} %forcing_hbm.1, bf16[3104,256]{1,0:T(8,128)(2,1)} %constant.12.clone.ca, bf16[512,512]{1,0:T(8,128)(2,1)} %constant.13.clone.cb, bf16[80,320]{1,0:T(8,128)(2,1)} %constant.14.clone.cc, ...), custom_call_target="tpu_custom_call" | custom-call | tf_op jit(solution)/shard_map/step/pallas_call | solution.py:579
  77.4 0.7 copy.16
  78.1 0.6 copy.17
